TPU v7x, 256 devices: a whole 4x4x8 slice. The times are simulated.
256 devices in a mesh: group: 8 (over x, core), ctx: 32 (over z, y).
Axes of the slice: x: 4, y: 4, z: 8, core: 2. Of those that a mesh axis runs over, the one named last changes fastest.
Arguments:
- series: bfloat16 [65536, 768], P(('group', 'ctx')), may hold values from -6 to 6
- recon_mask: int32 [65536], P(('group', 'ctx')), may hold values 0 or 1
- mask_token: bfloat16 [768], replicated, may hold values from -4 to 4
- packing_list: int32 [2048], P(('group', 'ctx')), may hold values from 0 to 7, as said below
- doc_ids: int32 [8, 8192], P('group', 'ctx'), may hold values from 0 to 3, never falling along the last dimension, each value on 1 to 5120 neighbouring positions
- norm_gain: bfloat16 [768], replicated, may hold values from 0.099609375 to 1.8984375
- w_query: bfloat16 [768, 768], replicated
- w_key: bfloat16 [768, 768], replicated
- w_value: bfloat16 [768, 768], replicated, may hold values from -0.21875 to 0.21875
- w_out: bfloat16 [768, 768], replicated, may hold values from -0.21875 to 0.21875
Outputs:
- encoded: bfloat16 [65536, 768], P(('group', 'ctx'))
Inputs may be any that keep to these rules, and one draw needn't show every extreme that they name: `packing_list`: the 8 consecutive entries of each arrival block (one device of the arrival layout) name every packed group exactly once.
All inputs are finite; a program needn't handle non-finite values. No bound on the sum of `recon_mask` on one device may be relied on, other than what follows from the above.
Results may differ from a plain program's by a relative error of at most 0.005.
Values may be sent and summed in bfloat16 or wider, within the bound.
A program may use at most 128 MiB of HBM per device.

v0:
```python
import math

import jax
import jax.numpy as jnp
from jax import lax
from jax.sharding import PartitionSpec as P

HEADS = 12
HD = 64


NEGATIVE = -1e30


def rms_normed(values, gain):
    widened = values.astype(jnp.float32)
    factor = lax.rsqrt(jnp.mean(widened * widened, axis=-1, keepdims=True) + 1e-06)
    return (widened * factor * gain.astype(jnp.float32)[None, :]).astype(jnp.bfloat16)


def softmax_update(carried, query, query_doc, key_rows, value_rows, key_doc):
    maxima, totals, running = carried
    key_count = key_rows.shape[0]
    head_query = query.reshape(query.shape[0], HEADS, HD)
    head_key = key_rows.reshape(key_count, HEADS, HD)
    head_value = value_rows.reshape(key_count, HEADS, HD)
    scores = jnp.einsum(
        "qhd,khd->hqk", head_query, head_key, preferred_element_type=jnp.float32
    ) * (1.0 / math.sqrt(HD))
    allowed = (query_doc[:, None] == key_doc[None, :])[None]
    scores = jnp.where(allowed, scores, NEGATIVE)
    newmax = jnp.maximum(maxima, jnp.max(scores, axis=-1))
    expo = jnp.where(allowed, jnp.exp(scores - newmax[..., None]), 0.0)
    factor = jnp.exp(maxima - newmax)
    totals = totals * factor + jnp.sum(expo, axis=-1)
    running = running * factor[..., None] + jnp.einsum(
        "hqk,khd->hqd", expo.astype(jnp.bfloat16), head_value, preferred_element_type=jnp.float32
    )
    return (newmax, totals, running)


def visit_tiles(carried, tile_source, project, query, query_doc):
    total_rows = tile_source[0].shape[0]
    tile_rows = math.gcd(total_rows, 512)
    tile_count = total_rows // tile_rows
    stacked = tuple(
        (member.reshape((tile_count, tile_rows) + member.shape[1:]) for member in tile_source)
    )

    def one_tile(status, tile_parts):
        tile_doc = tile_parts[-1].astype(jnp.int32)
        key_rows, value_rows = project(tile_parts)
        return (softmax_update(status, query, query_doc, key_rows, value_rows, tile_doc), None)

    carried, unused = lax.scan(one_tile, carried, stacked)
    return carried


def on_device(
    series, recon_mask, mask_token, packing_list, doc_ids, norm_gain, w_query, w_key, w_value, w_out
):
    groups = lax.axis_size("group")
    row_count, model_width = series.shape
    masked = jnp.where(recon_mask[:, None] == 1, mask_token[None, :], series)
    routing = (packing_list[None, :] == jnp.arange(groups, dtype=jnp.int32)[:, None]).astype(
        jnp.bfloat16
    )
    ordered = jnp.dot(
        routing, masked.reshape(groups, -1), preferred_element_type=jnp.float32
    ).astype(jnp.bfloat16)
    packed = lax.all_to_all(ordered, "group", split_axis=0, concat_axis=0, tiled=True).reshape(
        row_count, model_width
    )
    normed = rms_normed(packed, norm_gain)
    query = jnp.dot(normed, w_query, preferred_element_type=jnp.float32).astype(jnp.bfloat16)
    query_doc = doc_ids.reshape(-1)
    doc_wire = query_doc.astype(jnp.bfloat16)
    start_carry = (
        jnp.full((HEADS, row_count), NEGATIVE, jnp.float32),
        jnp.zeros((HEADS, row_count), jnp.float32),
        jnp.zeros((HEADS, row_count, HD), jnp.float32),
    )
    keys_local = jnp.dot(normed, w_key, preferred_element_type=jnp.float32).astype(jnp.bfloat16)
    values_local = jnp.dot(normed, w_value, preferred_element_type=jnp.float32).astype(jnp.bfloat16)

    def direct(tile_parts):
        return (tile_parts[0], tile_parts[1])

    maxima, totals, running = visit_tiles(
        start_carry,
        (
            lax.all_gather(keys_local, "ctx", axis=0, tiled=True),
            lax.all_gather(values_local, "ctx", axis=0, tiled=True),
            lax.all_gather(doc_wire, "ctx", axis=0, tiled=True),
        ),
        direct,
        query,
        query_doc,
    )
    attended = (
        (running / totals[..., None])
        .transpose(1, 0, 2)
        .reshape(row_count, model_width)
        .astype(jnp.bfloat16)
    )
    mixed = jnp.dot(attended, w_out, preferred_element_type=jnp.float32)
    out_packed = (packed.astype(jnp.float32) + mixed).astype(jnp.bfloat16)
    returned = lax.all_to_all(
        out_packed.reshape(groups, -1), "group", split_axis=0, concat_axis=0, tiled=True
    )
    arrival = jnp.dot(routing.T, returned, preferred_element_type=jnp.float32).astype(jnp.bfloat16)
    return arrival.reshape(row_count, model_width)


def solution(mesh):
    in_specs = (
        P(("group", "ctx"), None),
        P(("group", "ctx")),
        P(),
        P(("group", "ctx")),
        P("group", "ctx"),
        P(),
        P(),
        P(),
        P(),
        P(),
    )
    out_specs = P(("group", "ctx"), None)
    return jax.shard_map(
        on_device, mesh=mesh, in_specs=in_specs, out_specs=out_specs, check_vma=False
    )
```

profile of v0, /device:TPU:1, one launch (start us, length us, event | category | flops | bytes accessed | tf_op | source)
XLA Modules:
  0.0 465.0 jit_solution(6521077353694479750)
XLA Ops:
  12.0 6.6 %all-to-all-start = ((bf16[8,2,12288]{2,1,0:T(2,128)(2,1)}), bf16[8,2,12288]{2,1,0:T(2,128)(2,1)S(1)}, u32[]{:S(2)}, u32[]{:S(2)}) async-start(bf16[8,2,12288]{2,1,0:T(2,128)(2,1)} %reshape.102), calls=%async_computation | async-start | bytes 786432 | tf_op jit(solution)/shard_map/all_to_all | solution.py:71
  19.3 7.4 %all-to-all-done = bf16[8,2,12288]{2,1,0:T(2,128)(2,1)S(1)} async-done(((bf16[8,2,12288]{2,1,0:T(2,128)(2,1)}), bf16[8,2,12288]{2,1,0:T(2,128)(2,1)S(1)}, u32[]{:S(2)}, u32[]{:S(2)}) %all-to-all-start) | async-done | bytes 393248 | tf_op jit(solution)/shard_map/all_to_all | solution.py:71
  27.1 2.2 convert_reduce_fusion
  31.0 2.5 convolution_convert_fusion.4
  33.6 38.3 %all-gather = bf16[1,8192]{1,0:T(2,128)(2,1)S(1)} all-gather(bf16[1,256]{1,0:T(2,128)(2,1)S(1)} %convert_element_type.59), channel_id=2, replica_groups=mesh['group'=8,'ctx'=32] {'ctx'}, dimensions={1}, use_global_device_ids=true | all-gather | bytes 16896 | tf_op jit(solution)/shard_map/all_gather | solution.py:94
  72.0 1.7 convolution_convert_fusion.3
  74.7 76.3 %all-gather.6.cloned.1.call-done = bf16[8192,768]{1,0:T(8,128)(2,1)} async-done(((bf16[256,768]{1,0:T(8,128)(2,1)}), bf16[8192,768]{1,0:T(8,128)(2,1)}) %all-gather.6.cloned.1.call-update) | async-done | bytes 12582928 | tf_op jit(solution)/shard_map/all_gather | solution.py:93
  151.0 119.4 %all-gather.4.cloned.1.call-done = bf16[8192,768]{1,0:T(8,128)(2,1)} async-done(((bf16[256,768]{1,0:T(8,128)(2,1)}), bf16[8192,768]{1,0:T(8,128)(2,1)}) %all-gather.4.cloned.1.call-update) | async-done | bytes 12582928 | tf_op jit(solution)/shard_map/all_gather | solution.py:92
  270.3 166.1 %while.15 = (s32[]{:T(128)}, f32[12,256]{1,0:T(8,128)S(1)}, f32[12,256]{1,0:T(8,128)}, f32[12,256,64]{1,2,0:T(8,128)}, s32[1,256]{1,0:T(1,128)S(1)}, /*index=5*/...) while((s32[]{:T(128)}, f32[12,256]{1,0:T(8,128)S(1)}, ...), condition=%wide.region_4.5_spmd.clone, body=%wide.region_1.4_spmd.clone.sunk | while | flops 423837184 | bytes 39627148 | solution.py:55
  271.2 1.5 constant_dynamic-slice_fusion.3
  274.1 2.3 fusion.43
  276.5 1.5 fusion.44
  278.0 1.8 fusion.46
  281.5 1.5 constant_dynamic-slice_fusion.3
  284.5 2.3 fusion.43
  286.9 1.5 fusion.44
  288.4 1.8 fusion.46
  291.9 1.5 constant_dynamic-slice_fusion.3
  294.9 2.3 fusion.43
  297.2 1.5 fusion.44
  298.8 1.8 fusion.46
  302.3 1.5 constant_dynamic-slice_fusion.3
  305.3 2.3 fusion.43
  307.6 1.5 fusion.44
  309.2 1.8 fusion.46
  315.7 2.3 fusion.43
  318.0 1.5 fusion.44
  319.6 1.8 fusion.46
  326.1 2.3 fusion.43
  328.4 1.5 fusion.44
  330.0 1.8 fusion.46
  336.4 2.3 fusion.43
  338.8 1.5 fusion.44
  340.3 1.8 fusion.46
  346.8 2.3 fusion.43
  349.2 1.5 fusion.44
  350.7 1.8 fusion.46
  357.2 2.3 fusion.43
  359.5 1.5 fusion.44
  361.1 1.8 fusion.46
  367.6 2.3 fusion.43
  369.9 1.5 fusion.44
  371.5 1.8 fusion.46
  378.0 2.3 fusion.43
  380.3 1.5 fusion.44
  381.9 1.8 fusion.46
  388.4 2.3 fusion.43
  390.7 1.5 fusion.44
  392.3 1.8 fusion.46
  398.7 2.3 fusion.43
  401.1 1.5 fusion.44
  402.6 1.8 fusion.46
  409.1 2.3 fusion.43
  411.5 1.5 fusion.44
  413.0 1.8 fusion.46
  419.5 2.3 fusion.43
  421.8 1.5 fusion.44
  423.4 1.8 fusion.46
  429.9 2.3 fusion.43
  432.2 1.5 fusion.44
  433.8 1.8 fusion.46
  437.7 2.0 fusion.14
  439.9 3.0 reduce.4
  443.2 13.2 %all_to_all.22 = bf16[8,2,12288]{2,1,0:T(2,128)(2,1)S(1)} all-to-all(bf16[8,2,12288]{2,1,0:T(2,128)(2,1)S(1)} %reshape.104), channel_id=1, replica_groups=mesh['group'=8,'ctx'=32] {'group'}, dimensions={0} | all-to-all | bytes 786432 | tf_op jit(solution)/shard_map/all_to_all | solution.py:108
  (451 shorter events, 81.4 us)
Async XLA Ops:
  6.5 23.2 %copy-start = (bf16[768,768]{1,0:T(8,128)(2,1)S(1)}, bf16[768,768]{1,0:T(8,128)(2,1)}, u32[]{:S(2)}) copy-start(bf16[768,768]{1,0:T(8,128)(2,1)} %param.20) | copy-start | bytes 3538948
  10.9 22.6 %copy-start.10 = (s32[1,256]{1,0:T(1,128)S(1)}, s32[1,256]{1,0:T(1,128)}, u32[]{:S(2)}) copy-start(s32[1,256]{1,0:T(1,128)} %param.16) | copy-start | bytes 3076
  12.0 14.7 %all-to-all-start = ((bf16[8,2,12288]{2,1,0:T(2,128)(2,1)}), bf16[8,2,12288]{2,1,0:T(2,128)(2,1)S(1)}, u32[]{:S(2)}, u32[]{:S(2)}) async-start(bf16[8,2,12288]{2,1,0:T(2,128)(2,1)} %reshape.102), calls=%async_computation | async-start | bytes 786432 | tf_op jit(solution)/shard_map/all_to_all | solution.py:71
  18.6 132.4 %all-gather.6.cloned.1.call-start = ((), (), s32[]{:S(2)}) async-start(), calls=%async_computation.3 | async-start | bytes 12976128 | tf_op jit(solution)/shard_map/all_gather | solution.py:93
  29.4 240.9 %copy-start.3 = (f32[256,768]{1,0:T(8,128)}, f32[256,768]{1,0:T(8,128)S(1)}, u32[]{:S(2)}) copy-start(f32[256,768]{1,0:T(8,128)S(1)} %reshape.93) | copy-start | bytes 2359300
  31.0 239.4 %all-gather.4.cloned.1.call-start = ((), (), s32[]{:S(2)}) async-start(), calls=%async_computation.2 | async-start | bytes 12976128 | tf_op jit(solution)/shard_map/all_gather | solution.py:92
  272.9 3.5 copy-start.1
  274.1 3.8 copy-start.6
  274.1 3.9 copy-start.2
  274.1 3.9 copy-start.4
  283.3 3.5 copy-start.1
  284.5 3.8 copy-start.6
  284.5 3.9 copy-start.2
  284.5 3.9 copy-start.4
  293.7 3.5 copy-start.1
  294.9 3.8 copy-start.6
  294.9 3.9 copy-start.2
  294.9 3.9 copy-start.4
  305.3 3.8 copy-start.6
  305.3 3.9 copy-start.2
  305.3 3.9 copy-start.4
  315.7 3.8 copy-start.6
  315.7 3.9 copy-start.2
  315.7 3.9 copy-start.4
  326.1 3.8 copy-start.6
  326.1 3.9 copy-start.2
  326.1 3.9 copy-start.4
  335.2 3.5 copy-start.1
  336.4 3.8 copy-start.6
  336.4 3.9 copy-start.2
  336.4 3.9 copy-start.4
  345.6 3.5 copy-start.1
  346.8 3.8 copy-start.6
  346.8 3.9 copy-start.2
  346.8 3.9 copy-start.4
  356.0 3.5 copy-start.1
  357.2 3.8 copy-start.6
  357.2 3.9 copy-start.2
  357.2 3.9 copy-start.4
  366.4 3.5 copy-start.1
  367.6 3.8 copy-start.6
  367.6 3.9 copy-start.2
  367.6 3.9 copy-start.4
  376.8 3.5 copy-start.1
  378.0 3.8 copy-start.6
  378.0 3.9 copy-start.2
  378.0 3.9 copy-start.4
  387.2 3.5 copy-start.1
  388.4 3.8 copy-start.6
  388.4 3.9 copy-start.2
  388.4 3.9 copy-start.4
  398.7 3.8 copy-start.6
  398.7 3.9 copy-start.2
  398.7 3.9 copy-start.4
  409.1 3.8 copy-start.6
  409.1 3.9 copy-start.2
  409.1 3.9 copy-start.4
  419.5 3.8 copy-start.6
  419.5 3.9 copy-start.2
  419.5 3.9 copy-start.4
  429.9 3.8 copy-start.6
  429.9 3.9 copy-start.2
  429.9 3.9 copy-start.4
  436.5 20.2 %copy-start.12 = (s32[8]{0:T(128)S(1)}, s32[8]{0:T(128)}, u32[]{:S(2)}) copy-start(s32[8]{0:T(128)} %param.15) | copy-start | bytes 100
  (87 other events, 191.7 us)
Sparse Core Ops, SparseCore 0:
  31.1 119.8 all-gather.5
  153.5 116.7 all-gather.3
where the time goes:
time: 466 us; the launch traced here: 465 us
  waiting for transfers between devices  203 us (44%)
  matrix products  74.4 us (16%)
  local copies, waits for them, and re-layouts  66.3 us (14%)
  blocking collectives  51.4 us (11%)
  other arithmetic  47.2 us (10%)
  between operations  13.6 us (3%)
  starting transfers between devices  6.64 us (1%)
    all_gather x1, waiting for transfers between devices, on_device(): lax.all_gather(keys_local, 'ctx', axis=0, tiled=True)  119 us
    all_gather x1, waiting for transfers between devices, on_device(): lax.all_gather(values_local, 'ctx', axis=0, tiled=True)  76.3 us
    dynamic_slice x48, local copies, waits for them, and re-layouts, visit_tiles(): carried, unused = lax.scan(one_tile, carried, stacked)  47 us
    all_gather x1, blocking collectives, on_device(): lax.all_gather(doc_wire, 'ctx', axis=0, tiled=True)  38.3 us
    dot_general x16, matrix products, softmax_update(): jnp.einsum('qhd,khd->hqk', head_query, head_key, preferred_element_type=j...  36.8 us
    dot_general x16, matrix products, softmax_update(): jnp.einsum('hqk,khd->hqd', expo.astype(jnp.bfloat16), head_value, preferr...  28.7 us
    reduce_sum x16, other arithmetic, softmax_update(): totals = totals * factor + jnp.sum(expo, axis=-1)  23.7 us
    while x304, local copies, waits for them, and re-layouts  14.3 us
  transfers between devices with their start and end apart: 3, of which 3 were waited for; matrix products, arithmetic and copies ran while one was open for 1% of the time, Pallas kernels for 0%

commit v1 on v0

v1 whole, which is shorter than its diff:
```python
import functools
import math

import jax
import jax.numpy as jnp
from jax import lax
from jax.experimental import pallas as pl
from jax.experimental.pallas import tpu as pltpu
from jax.sharding import PartitionSpec as P

D = 768
HEADS = 12
HD = 64
BLK = 32
N_GROUP = 8
N_CTX = 32
N_Z = 8
N_Y = 4
TRIPLES = 4
PER = 3
QROWS = 48
ROWS = N_CTX * BLK
NEGATIVE = -1e30
SCALE = math.log2(math.e) / math.sqrt(HD)
TQ = 256
KC = 4
MESH = pl.DeviceIdType.MESH


def low_half(shape):
    return lax.broadcasted_iota(jnp.int32, shape, len(shape) - 1) < HD


def swap(x):
    return pltpu.roll(x, HD, 1)


def join(a, b):
    return jnp.where(low_half(a.shape), a, b)


def masked_rows(series_ref, recon_ref, token_ref):
    return jnp.where(
        recon_ref[...] == 1, token_ref[...].astype(jnp.float32), series_ref[...].astype(jnp.float32)
    )


def project_kernel(
    packing_ref, series_ref, recon_ref, token_ref, doc_ref, gain_ref, wq_ref, wk_ref, wv_ref,
    kv_ref, q_ref, count_ref,
):
    x = masked_rows(series_ref, recon_ref, token_ref)
    factor = lax.rsqrt(jnp.mean(x * x, axis=-1, keepdims=True) + 1e-06)
    normed = (x * factor * gain_ref[...].astype(jnp.float32)).astype(jnp.bfloat16)
    ids = doc_ref[...]
    lane = lax.broadcasted_iota(jnp.int32, (8, 128), 1)
    count = jnp.zeros((8, 128), jnp.int32)
    for d in range(3):
        below = jnp.sum((ids <= d).astype(jnp.float32), axis=1, keepdims=True).astype(jnp.int32)
        count = jnp.where(lane == d, below, count)
    count_ref[...] = count

    def project(w_ref):
        return jnp.dot(normed, w_ref[...], preferred_element_type=jnp.float32)

    def piece(values, k):
        return values[k * BLK : (k + 1) * BLK]

    key, value = project(wk_ref), project(wv_ref)
    for m in range(HEADS // 2):
        kp, vp = key[:, m * 128 : (m + 1) * 128], value[:, m * 128 : (m + 1) * 128]
        for head, kv in ((2 * m, join(kp, swap(vp))), (2 * m + 1, join(swap(kp), vp))):
            kv = kv.astype(jnp.bfloat16)
            for k in range(N_GROUP):
                kv_ref[packing_ref[k] * TRIPLES + head // PER, head % PER] = piece(kv, k)
    query = project(wq_ref) * SCALE
    for t in range(TRIPLES):
        pair = [query[:, m * 128 : (m + 1) * 128] for m in (3 * t // 2, 3 * t // 2 + 1)]
        if t % 2 == 0:
            first, last = pair[0], pair[1]
        else:
            first, last = join(swap(pair[0]), swap(pair[1])), swap(pair[1])
        first = first.astype(jnp.bfloat16)
        swapped = swap(last)
        for k in range(N_GROUP):
            to = packing_ref[k] * TRIPLES + t
            q_ref[to, 0:BLK] = piece(first, k)
            half = join(last[k * BLK : k * BLK + 16], swapped[k * BLK + 16 : (k + 1) * BLK])
            q_ref[to, BLK:QROWS] = half.astype(jnp.bfloat16)


def project(series, recon, token, packing, docs, gain, wq, wk, wv):
    vmem = pl.BlockSpec(memory_space=pltpu.VMEM)
    return pl.pallas_call(
        project_kernel,
        out_shape=(
            jax.ShapeDtypeStruct((N_CTX, PER, BLK, 128), jnp.bfloat16),
            jax.ShapeDtypeStruct((N_CTX, QROWS, 128), jnp.bfloat16),
            jax.ShapeDtypeStruct((8, 128), jnp.int32),
        ),
        in_specs=[pl.BlockSpec(memory_space=pltpu.SMEM)] + [vmem] * 8,
        out_specs=(vmem, vmem, vmem),
        compiler_params=pltpu.CompilerParams(vmem_limit_bytes=48 << 20),
        name="project",
    )(packing, series, recon, token, docs, gain, wq, wk, wv)


def step_z(i):
    return lax.rem(N_Z + (1 - 2 * lax.rem(i + 1, 2)) * ((i + 1) // 2), N_Z)


def spread_kernel(
    kv_ref, q_ref, count_ref, all_ref, qout_ref, total_ref,
    counts, kv_send, kv_recv, q_send, q_recv, c_send, c_recv, self_sem,
    x_send, near_recv, half_recv, pair_recv, t_send, t_recv,
):
    s = lax.axis_index("group")
    c = lax.axis_index("ctx")
    z, y = c // N_Y, lax.rem(c, N_Y)
    partner = s + 1 - 2 * lax.rem(s, 2)
    right, left, across = lax.rem(s + 2, N_GROUP), lax.rem(s + 6, N_GROUP), lax.rem(s + 4, N_GROUP)
    bar = pltpu.get_barrier_semaphore()

    def greet(o, carry):
        pl.semaphore_signal(
            bar, inc=1, device_id=(s, lax.rem(c + o, N_CTX)), device_id_type=MESH
        )
        return carry

    lax.fori_loop(1, N_CTX, greet, 0)
    for other in (partner, right, left):
        pl.semaphore_signal(bar, inc=1, device_id=(other, c), device_id_type=MESH)
    pl.semaphore_wait(bar, N_CTX - 1 + 3)

    def rows_of(d):
        return pl.ds(pl.multiple_of(d * BLK, BLK), BLK)

    def send_kv(d):
        return pltpu.make_async_remote_copy(
            src_ref=kv_ref.at[d], dst_ref=all_ref.at[:, s, rows_of(c), :],
            send_sem=kv_send.at[d], recv_sem=kv_recv.at[c],
            device_id=(s, d), device_id_type=MESH,
        )

    def arrive_kv(d):
        return pltpu.make_async_remote_copy(
            src_ref=kv_ref.at[d], dst_ref=all_ref.at[:, s, rows_of(d), :],
            send_sem=kv_send.at[d], recv_sem=kv_recv.at[d],
            device_id=(s, d), device_id_type=MESH,
        )

    def send_q(d, at):
        return pltpu.make_async_remote_copy(
            src_ref=q_ref.at[d], dst_ref=qout_ref.at[at],
            send_sem=q_send.at[d], recv_sem=q_recv.at[at],
            device_id=(s, d), device_id_type=MESH,
        )

    def send_count(d, at):
        return pltpu.make_async_remote_copy(
            src_ref=count_ref, dst_ref=counts.at[at],
            send_sem=c_send.at[d], recv_sem=c_recv.at[at],
            device_id=(s, d), device_id_type=MESH,
        )

    def other(i, yy):
        return lax.rem(z + step_z(i), N_Z) * N_Y + lax.rem(y + yy, N_Y)

    own_kv = pltpu.make_async_copy(kv_ref.at[c], all_ref.at[:, s, rows_of(c), :], self_sem.at[0])
    own_q = pltpu.make_async_copy(q_ref.at[c], qout_ref.at[c], self_sem.at[1])
    own_count = pltpu.make_async_copy(count_ref, counts.at[c], self_sem.at[2])
    own_kv.start()
    own_q.start()
    own_count.start()
    for yy in range(1, N_Y):
        send_kv(other(0, yy)).start()

    def start_plane(i, carry):
        for yy in range(N_Y):
            send_kv(other(i, yy)).start()
        return carry

    lax.fori_loop(1, N_Z, start_plane, 0)

    def start_rest(o, carry):
        d = lax.rem(c + o, N_CTX)
        send_count(d, c).start()
        send_q(d, c).start()
        return carry

    lax.fori_loop(1, N_CTX, start_rest, 0)

    def plane(i):
        return lax.rem(z + N_Z - step_z(i), N_Z)

    def hop(slot, i, to, kind, recv, half=None):
        first, size = plane(i) * 128, 128
        if half is not None:
            first, size = first + half * 64, 64
        part = all_ref.at[:, slot, pl.ds(pl.multiple_of(first, 64), size), :]
        return pltpu.make_async_remote_copy(
            src_ref=part, dst_ref=part, send_sem=x_send.at[kind, i], recv_sem=recv,
            device_id=(to, c), device_id_type=MESH,
        )

    def own_right(i):
        return hop(s, i, right, 0, near_recv.at[0, i])

    def own_left(i):
        return hop(s, i, left, 1, near_recv.at[1, i])

    def own_pair(i):
        return hop(s, i, partner, 2, pair_recv.at[0, i])

    def left_on(i):
        return hop(left, i, right, 3, half_recv.at[0, i], half=0)

    def right_on(i):
        return hop(right, i, left, 4, half_recv.at[1, i], half=1)

    def left_pair(i):
        return hop(left, i, partner, 5, pair_recv.at[1, i])

    def right_pair(i):
        return hop(right, i, partner, 6, pair_recv.at[2, i])

    def across_pair(i):
        return hop(across, i, partner, 7, pair_recv.at[3, i])

    def from_left(i):
        return hop(left, i, left, 0, near_recv.at[0, i])

    def from_right(i):
        return hop(right, i, right, 1, near_recv.at[1, i])

    def across_from_left(i):
        return hop(across, i, left, 3, half_recv.at[0, i], half=0)

    def across_from_right(i):
        return hop(across, i, right, 4, half_recv.at[1, i], half=1)

    def send_own(i):
        own_right(i).start()
        own_left(i).start()
        own_pair(i).start()

    def send_near(i):
        from_left(i).wait_recv()
        left_on(i).start()
        left_pair(i).start()
        from_right(i).wait_recv()
        right_on(i).start()
        right_pair(i).start()

    def send_across(i):
        across_from_left(i).wait_recv()
        across_from_right(i).wait_recv()
        across_pair(i).start()

    own_kv.wait()
    for yy in range(1, N_Y):
        arrive_kv(z * N_Y + lax.rem(y + yy, N_Y)).wait_recv()
    send_own(0)

    def arrive_plane(i):
        for yy in range(N_Y):
            arrive_kv(plane(i) * N_Y + yy).wait_recv()

    arrive_plane(1)
    send_own(1)
    send_near(0)

    def step(i, carry):
        arrive_plane(i)
        send_own(i)
        send_near(i - 1)
        send_across(i - 2)
        return carry

    lax.fori_loop(2, N_Z, step, 0)
    send_near(N_Z - 1)
    send_across(N_Z - 2)

    own_count.wait()

    def arrive_count(o, carry):
        send_count(lax.rem(c + o, N_CTX), lax.rem(c + o, N_CTX)).wait_recv()
        return carry

    lax.fori_loop(1, N_CTX, arrive_count, 0)
    total_ref[s] = jnp.sum(counts[...], axis=0)

    def pass_total(slot, to, kind):
        return pltpu.make_async_remote_copy(
            src_ref=total_ref.at[slot], dst_ref=total_ref.at[slot],
            send_sem=t_send.at[kind], recv_sem=t_recv.at[kind],
            device_id=(to, c), device_id_type=MESH,
        )

    sends = [pass_total(s, right, 0), pass_total(s, left, 1), pass_total(s, partner, 2)]
    for one in sends:
        one.start()
    send_across(N_Z - 1)
    pass_total(left, left, 0).wait_recv()
    later = [pass_total(left, right, 3), pass_total(left, partner, 4)]
    pass_total(right, right, 1).wait_recv()
    later.append(pass_total(right, partner, 5))
    for one in later:
        one.start()
    pass_total(across, left, 3).wait_recv()
    last = pass_total(across, partner, 6)
    last.start()
    back = lax.rem(partner + 6, N_GROUP)
    ahead = lax.rem(partner + 2, N_GROUP)
    beyond = lax.rem(partner + 4, N_GROUP)
    pass_total(partner, partner, 2).wait_recv()
    pass_total(back, partner, 4).wait_recv()
    pass_total(ahead, partner, 5).wait_recv()
    pass_total(beyond, partner, 6).wait_recv()
    for one in sends + later + [last]:
        one.wait_send()

    own_q.wait()

    def finish(o, carry):
        d = lax.rem(c + o, N_CTX)
        send_q(d, d).wait_recv()
        send_q(d, c).wait_send()
        send_count(d, c).wait_send()
        send_kv(d).wait_send()
        return carry

    lax.fori_loop(1, N_CTX, finish, 0)

    def finish_hops(i, carry):
        for sent in (own_right, own_left, own_pair, left_on, right_on, left_pair, right_pair, across_pair):
            sent(i).wait_send()
        for n, slot in enumerate((partner, back, ahead, beyond)):
            hop(slot, i, partner, 2, pair_recv.at[n, i]).wait_recv()
        return carry

    lax.fori_loop(0, N_Z, finish_hops, 0)


def spread(kv, q, count):
    anywhere = pl.BlockSpec(memory_space=pl.ANY)
    vmem = pl.BlockSpec(memory_space=pltpu.VMEM)
    dma = pltpu.SemaphoreType.DMA
    return pl.pallas_call(
        spread_kernel,
        out_shape=(
            jax.ShapeDtypeStruct((PER, N_GROUP, ROWS, 128), jnp.bfloat16),
            jax.ShapeDtypeStruct((N_CTX, QROWS, 128), jnp.bfloat16),
            jax.ShapeDtypeStruct((N_GROUP, 8, 128), jnp.int32),
        ),
        in_specs=[anywhere, anywhere, vmem],
        out_specs=(anywhere, anywhere, vmem),
        scratch_shapes=[
            pltpu.VMEM((N_CTX, 8, 128), jnp.int32),
            dma((N_CTX,)), dma((N_CTX,)), dma((N_CTX,)), dma((N_CTX,)), dma((N_CTX,)), dma((N_CTX,)),
            dma((3,)), dma((8, N_Z)), dma((2, N_Z)), dma((2, N_Z)), dma((4, N_Z)), dma((7,)), dma((7,)),
        ],
        compiler_params=pltpu.CompilerParams(collective_id=0, has_side_effects=True),
        name="spread",
    )(kv, q, count)


def attend_kernel(total_ref, q_ref, kv_ref, out_ref, qs, v1):
    h = pl.program_id(0)
    s = lax.axis_index("group")
    g = lax.axis_index("ctx") // N_Y
    starts = [total_ref[g, 0, d] for d in range(3)]
    zero = jnp.zeros((), jnp.float32)

    @pl.when(h == 0)
    def _():
        q = q_ref[:, 0:BLK, :].reshape(ROWS, 128).astype(jnp.float32)
        qs[...] = join(q, zero).astype(jnp.bfloat16).reshape(N_CTX, BLK, 128)

    @pl.when(h == 1)
    def _():
        q = q_ref[:, 0:BLK, :].reshape(ROWS, 128).astype(jnp.float32)
        qs[...] = join(swap(q), zero).astype(jnp.bfloat16).reshape(N_CTX, BLK, 128)

    @pl.when(h == 2)
    def _():
        q = q_ref[:, BLK:QROWS, :].reshape(ROWS // 2, 128).astype(jnp.float32)
        qs[:, 0:16] = join(q, zero).astype(jnp.bfloat16).reshape(N_CTX, 16, 128)
        qs[:, 16:32] = join(swap(q), zero).astype(jnp.bfloat16).reshape(N_CTX, 16, 128)

    one = jnp.ones((), jnp.bfloat16)
    for n in range(N_GROUP):
        v1[n] = jnp.where(low_half((ROWS, 128)), one, kv_ref[0, n])

    span = TQ // BLK * 256
    keys_n = KC * 256

    def doc_of(pos):
        return sum((pos >= st).astype(jnp.int32) for st in starts)

    for t in range(ROWS // TQ):
        p0, p1 = t * span, (t + 1) * span - 1
        lo, single, hi = jnp.int32(0), jnp.int32(0), jnp.int32(N_CTX * 256)
        for st in starts:
            lo = jnp.maximum(lo, jnp.where(st <= p0, st, 0))
            single = jnp.maximum(single, jnp.where(st <= p1, st, 0))
            hi = jnp.minimum(hi, jnp.where(st > p1, st, N_CTX * 256))
        blocks = TQ // BLK
        qt = qs[t * blocks : (t + 1) * blocks].reshape(TQ, 128)
        i = lax.broadcasted_iota(jnp.int32, (TQ, 1), 0)
        q_doc = doc_of((t * blocks + i // BLK) * 256 + s * BLK + i % BLK)

        def tile(kb, carry, masked):
            m, acc = carry
            rows = pl.ds(pl.multiple_of(kb * (KC * BLK), KC * BLK), KC * BLK)
            keys = kv_ref[0, :, rows, :].reshape(keys_n, 128)
            sc = lax.dot_general(
                qt, keys, (((1,), (1,)), ((), ())), preferred_element_type=jnp.float32
            )
            if masked:
                r = lax.broadcasted_iota(jnp.int32, (1, keys_n), 1)
                at = r % (KC * BLK)
                pos = (kb * KC + at // BLK) * 256 + (r // (KC * BLK)) * BLK + at % BLK
                sc = jnp.where(q_doc == doc_of(pos), sc, NEGATIVE)
            new = jnp.maximum(m, jnp.max(sc, axis=1, keepdims=True))
            p = jnp.exp2(sc - new).astype(jnp.bfloat16)
            acc = acc * jnp.exp2(m - new) + jnp.dot(
                p, v1[:, rows, :].reshape(keys_n, 128), preferred_element_type=jnp.float32
            )
            return new, acc

        def body(kb, carry):
            clear = (lo == single) & (kb * keys_n >= lo) & ((kb + 1) * keys_n <= hi)
            return lax.cond(
                clear,
                lambda: tile(kb, carry, False),
                lambda: tile(kb, carry, True),
            )

        m, acc = lax.fori_loop(
            lo // keys_n,
            (hi + keys_n - 1) // keys_n,
            body,
            (jnp.full((TQ, 1), NEGATIVE, jnp.float32), jnp.zeros((TQ, 128), jnp.float32)),
        )
        o = acc / swap(acc)

        here = slice(t * blocks, (t + 1) * blocks)

        @pl.when(h == 0)
        def _():
            out_ref[here, 0:BLK] = swap(o).astype(jnp.bfloat16).reshape(blocks, BLK, 128)

        @pl.when(h == 1)
        def _():
            before = out_ref[here, 0:BLK].reshape(TQ, 128)
            out_ref[here, 0:BLK] = join(before, o.astype(jnp.bfloat16)).reshape(blocks, BLK, 128)

        @pl.when(h == 2)
        def _():
            o3 = o.reshape(blocks, BLK, 128)
            first, second = o3[:, 0:16].reshape(TQ // 2, 128), o3[:, 16:32].reshape(TQ // 2, 128)
            both = join(swap(first), second).astype(jnp.bfloat16)
            out_ref[here, BLK:QROWS] = both.reshape(blocks, 16, 128)


def attend(total, q, kv):
    return pl.pallas_call(
        attend_kernel,
        out_shape=jax.ShapeDtypeStruct((N_CTX, QROWS, 128), jnp.bfloat16),
        grid=(PER,),
        in_specs=[
            pl.BlockSpec(memory_space=pltpu.SMEM),
            pl.BlockSpec((N_CTX, QROWS, 128), lambda h: (0, 0, 0)),
            pl.BlockSpec((1, N_GROUP, ROWS, 128), lambda h: (h, 0, 0, 0)),
        ],
        out_specs=pl.BlockSpec((N_CTX, QROWS, 128), lambda h: (0, 0, 0)),
        scratch_shapes=[
            pltpu.VMEM((N_CTX, BLK, 128), jnp.bfloat16),
            pltpu.VMEM((N_GROUP, ROWS, 128), jnp.bfloat16),
        ],
        compiler_params=pltpu.CompilerParams(
            vmem_limit_bytes=56 << 20, dimension_semantics=("arbitrary",)
        ),
        name="attend",
    )(total, q, kv)


def finish_kernel(packing_ref, att_ref, series_ref, recon_ref, token_ref, w_ref, out_ref, lhs, w2):
    order = [PER * t + n for t in range(TRIPLES) for n in range(2)] + [2, 5, 8, 11]
    for n, head in enumerate(order):
        w2[n * HD : (n + 1) * HD, :] = w_ref[head * HD : (head + 1) * HD, :]
    for k in range(N_GROUP):
        g = packing_ref[k]
        rows = slice(k * BLK, (k + 1) * BLK)
        for t in range(TRIPLES):
            lhs[rows, t * 128 : (t + 1) * 128] = att_ref[g * TRIPLES + t, 0:BLK]
        for n in range(2):
            a = att_ref[g * TRIPLES + 2 * n, BLK:QROWS].astype(jnp.float32)
            b = att_ref[g * TRIPLES + 2 * n + 1, BLK:QROWS].astype(jnp.float32)
            cols = slice((TRIPLES + n) * 128, (TRIPLES + n + 1) * 128)
            lhs[k * BLK : k * BLK + 16, cols] = join(a, swap(b)).astype(jnp.bfloat16)
            lhs[k * BLK + 16 : (k + 1) * BLK, cols] = join(swap(a), b).astype(jnp.bfloat16)
    mixed = jnp.dot(lhs[...], w2[...], preferred_element_type=jnp.float32)
    out_ref[...] = (masked_rows(series_ref, recon_ref, token_ref) + mixed).astype(jnp.bfloat16)


def finish(packing, att, series, recon, token, w_out):
    vmem = pl.BlockSpec(memory_space=pltpu.VMEM)
    return pl.pallas_call(
        finish_kernel,
        out_shape=jax.ShapeDtypeStruct(series.shape, jnp.bfloat16),
        in_specs=[pl.BlockSpec(memory_space=pltpu.SMEM)] + [vmem] * 5,
        out_specs=vmem,
        scratch_shapes=[pltpu.VMEM((N_GROUP * BLK, D), jnp.bfloat16), pltpu.VMEM((D, D), jnp.bfloat16)],
        compiler_params=pltpu.CompilerParams(vmem_limit_bytes=48 << 20),
        name="finish",
    )(packing, att, series, recon, token, w_out)


def on_device(
    series, recon_mask, mask_token, packing_list, doc_ids, norm_gain, w_query, w_key, w_value, w_out
):
    recon = recon_mask.reshape(-1, 1)
    token = mask_token.reshape(1, -1)
    kv, q, count = project(
        series, recon, token, packing_list, doc_ids, norm_gain.reshape(1, -1), w_query, w_key, w_value
    )
    all_kv, q_rows, total = spread(kv, q, count)
    att = attend(total, q_rows, all_kv)
    back = lax.all_to_all(att, "ctx", split_axis=0, concat_axis=0, tiled=True)
    return finish(packing_list, back, series, recon, token, w_out)


def solution(mesh):
    split = P(("group", "ctx"))
    in_specs = (
        P(("group", "ctx"), None), split, P(), split, P("group", "ctx"), P(), P(), P(), P(), P(),
    )
    return jax.shard_map(
        on_device, mesh=mesh, in_specs=in_specs, out_specs=P(("group", "ctx"), None), check_vma=False
    )
```

time: 466 us -> 151 us (0.32)
  waiting for transfers between devices: 203 us -> 0 us
  Pallas kernels: 0 us -> 122 us
  matrix products: 74.4 us -> 0 us
  local copies, waits for them, and re-layouts: 66.3 us -> 10.6 us
  other arithmetic: 47.2 us -> 0 us
  blocking collectives: 51.4 us -> 18.3 us
  between operations: 13.6 us -> 0.08 us
  starting transfers between devices: 6.64 us -> 0 us
    all_gather x2 -> x0, waiting for transfers between devices: 196 us -> none  [the longest x1 119 us: on_device(): lax.all_gather(keys_local, 'ctx', axis=0, tiled=True)]
    pallas_call x0 -> x4, Pallas kernels: none -> 122 us  [the longest x1 59 us: spread(): pl.pallas_call(spread_kernel, out_shape=(jax.ShapeDtypeStruct((PER, N_GRO...]
    dot_general x38 -> x0, matrix products: 74.4 us -> none  [the longest x16 36.8 us: softmax_update(): jnp.einsum('qhd,khd->hqk', head_query, head_key, preferred_element_type=j...]
    dynamic_slice x48 -> x0, local copies, waits for them, and re-layouts: 47 us -> none  [visit_tiles(): carried, unused = lax.scan(one_tile, carried, stacked)]
    all_gather x1 -> x0, blocking collectives: 38.3 us -> none  [on_device(): lax.all_gather(doc_wire, 'ctx', axis=0, tiled=True)]
    reduce_sum x17 -> x0, other arithmetic: 23.8 us -> none  [the longest x16 23.7 us: softmax_update(): totals = totals * factor + jnp.sum(expo, axis=-1)]
    while x304 -> x0, local copies, waits for them, and re-layouts: 14.3 us -> none
    eq x17 -> x0, other arithmetic: 13.6 us -> none  [the longest x16 12.8 us: softmax_update(): allowed = (query_doc[:, None] == key_doc[None, :])[None]]
  transfers between devices with their start and end apart: 3 -> 0, of which waited for: 3 -> 0; matrix products, arithmetic and copies ran while one was open for 1% -> 0% of each run, Pallas kernels for 0% -> 0%
where the time goes in v1:
time: 151 us
  Pallas kernels  122 us (81%)
  blocking collectives  18.3 us (12%)
  local copies, waits for them, and re-layouts  10.6 us (7%)
    pallas_call x1, Pallas kernels, spread(): pl.pallas_call(spread_kernel, out_shape=(jax.ShapeDtypeStruct((PER, N_GRO...  59 us
    pallas_call x1, Pallas kernels, attend(): pl.pallas_call(attend_kernel, out_shape=jax.ShapeDtypeStruct((N_CTX, QROW...  58.8 us
    all_to_all x1, blocking collectives, on_device(): back = lax.all_to_all(att, 'ctx', split_axis=0, concat_axis=0, tiled=True)  18.3 us
    unnamed x24, local copies, waits for them, and re-layouts  8.38 us

profile of v1, /device:TPU:1, one launch (start us, length us, event | category | flops | bytes accessed | tf_op | source)
XLA Modules:
  0.0 150.6 jit_solution(2218092268408608721)
XLA Ops:
  0.0 0.7 reshape.10.token_ref
  0.7 0.7 reshape.11.gain_ref
  1.4 0.8 copy.11.recon_ref
  2.2 0.0 copy-start
  2.2 1.0 copy-done
  3.2 0.0 copy-start.3
  3.2 1.3 copy-done.3
  4.5 0.0 copy-start.4
  4.5 1.3 copy-done.4
  5.7 0.0 copy-start.5
  5.7 1.3 copy-done.5
  7.0 0.0 copy-start.9
  7.0 0.7 copy-done.9
  7.7 0.0 copy-start.11
  7.7 0.7 copy-done.11
  8.3 2.1 %project.1 = (bf16[32,3,32,128]{3,2,1,0:T(8,128)(2,1)S(1)}, bf16[32,48,128]{2,1,0:T(8,128)(2,1)S(1)}, s32[8,128]{1,0:T(8,128)S(1)}) custom-call(s32[8]{0:T(128)S(1)} %copy-done.9, bf16[256,768]{1,0:T(8,128)(2,1)S(1)} %copy-done, s32[256,1]{1,0:T(8,128)S(1)} %copy.11.recon_ref, bf16[1,768]{1,0:T(2,128)(2,1)S(1)} %reshape.10.token_ref, ...), custom_call_target="tpu_custom_call" | custom-call | tf_op jit(solution)/shard_map/project/pallas_call | solution.py:94
  10.4 0.0 copy-start.6
  10.4 0.9 copy-done.6
  11.3 0.0 copy-start.7
  11.3 0.7 copy-done.7
  12.1 0.0 copy-start.8
  12.1 0.6 copy-done.8
  12.7 59.0 %spread.1 = (bf16[3,8,1024,128]{3,2,1,0:T(8,128)(2,1)}, bf16[32,48,128]{2,1,0:T(8,128)(2,1)}, s32[8,8,128]{2,1,0:T(8,128)}) custom-call(bf16[32,3,32,128]{3,2,1,0:T(8,128)(2,1)} %copy-done.6, bf16[32,48,128]{2,1,0:T(8,128)(2,1)} %copy-done.7, s32[8,128]{1,0:T(8,128)} %copy-done.8), custom_call_target="tpu_custom_call" | custom-call | tf_op jit(solution)/shard_map/spread/pallas_call | solution.py:349
  71.7 0.0 copy-start.1
  71.7 0.0 copy-start.2
  71.7 0.0 copy-start.10
  71.7 58.8 %attend.1 = bf16[32,48,128]{2,1,0:T(8,128)(2,1)} custom-call(s32[8,8,128]{2,1,0:T(8,128)} %get-tuple-element.14.total_ref, bf16[32,48,128]{2,1,0:T(8,128)(2,1)} %get-tuple-element.15.q_ref, bf16[3,8,1024,128]{3,2,1,0:T(8,128)(2,1)} %get-tuple-element.16.kv_ref), custom_call_target="tpu_custom_call" | custom-call | tf_op jit(solution)/shard_map/attend/pallas_call | solution.py:468
  130.5 18.3 %all_to_all.5.att_ref = bf16[32,48,128]{2,1,0:T(8,128)(2,1)S(1)} all-to-all(bf16[32,48,128]{2,1,0:T(8,128)(2,1)} %attend.1), channel_id=1, replica_groups=mesh['group'=8,'ctx'=32] {'ctx'}, dimensions={0} | all-to-all | bytes 786432 | tf_op jit(solution)/shard_map/all_to_all | solution.py:531
  148.8 0.0 copy-done.1
  148.8 0.0 copy-done.2
  148.8 0.0 copy-done.10
  148.8 1.8 %finish.1 = bf16[256,768]{1,0:T(8,128)(2,1)} custom-call(s32[8]{0:T(128)S(1)} %copy-done.10, bf16[32,48,128]{2,1,0:T(8,128)(2,1)S(1)} %all_to_all.5.att_ref, bf16[256,768]{1,0:T(8,128)(2,1)S(1)} %copy-done.1, s32[256,1]{1,0:T(8,128)S(1)} %copy.11.recon_ref, bf16[1,768]{1,0:T(2,128)(2,1)S(1)} %reshape.10.token_ref, bf16[768,768]{1,0:T(8,128)(2,1)S(1)} %copy-done.2), custom_call_target="tpu_custom_call" | custom-call | tf_op jit(solution)/shard_map/finish/pallas_call | solution.py:510
Async XLA Ops:
  2.2 1.0 copy-start
  3.2 1.3 copy-start.3
  4.5 1.3 copy-start.4
  5.7 1.3 copy-start.5
  7.0 0.7 copy-start.9
  7.7 0.7 copy-start.11
  10.4 0.9 copy-start.6
  11.3 0.7 copy-start.7
  12.1 0.6 copy-start.8
  71.7 77.1 %copy-start.1 = (bf16[256,768]{1,0:T(8,128)(2,1)S(1)}, bf16[256,768]{1,0:T(8,128)(2,1)}, u32[]{:S(2)}) copy-start(bf16[256,768]{1,0:T(8,128)(2,1)} %series_ref.3) | copy-start | bytes 1179652
  71.7 77.1 %copy-start.2 = (bf16[768,768]{1,0:T(8,128)(2,1)S(1)}, bf16[768,768]{1,0:T(8,128)(2,1)}, u32[]{:S(2)}) copy-start(bf16[768,768]{1,0:T(8,128)(2,1)} %w_ref.1) | copy-start | bytes 3538948
  71.7 77.1 %copy-start.10 = (s32[8]{0:T(128)S(1)}, s32[8]{0:T(128)}, u32[]{:S(2)}) copy-start(s32[8]{0:T(128)} %packing_ref.3) | copy-start | bytes 100

commit v2 on v1

v2 whole, which is shorter than its diff:
```python
import functools
import math

import jax
import jax.numpy as jnp
from jax import lax
from jax.experimental import pallas as pl
from jax.experimental.pallas import tpu as pltpu
from jax.sharding import PartitionSpec as P

D = 768
HEADS = 12
HD = 64
BLK = 32
N_GROUP = 8
N_CTX = 32
N_Z = 8
N_Y = 4
TRIPLES = 4
PER = 3
QROWS = 48
ROWS = N_CTX * BLK
NEGATIVE = -1e30
DOCS = 4
BOUND = 100.0
SCALE = math.log2(math.e) / math.sqrt(HD)
TQ = 256
KC = 4
MESH = pl.DeviceIdType.MESH


def low_half(shape):
    return lax.broadcasted_iota(jnp.int32, shape, len(shape) - 1) < HD


def swap(x):
    return pltpu.roll(x, HD, 1)


def join(a, b):
    return jnp.where(low_half(a.shape), a, b)


def masked_rows(series_ref, recon_ref, token_ref):
    return jnp.where(
        recon_ref[...] == 1, token_ref[...].astype(jnp.float32), series_ref[...].astype(jnp.float32)
    )


def project_kernel(
    packing_ref, series_ref, recon_ref, token_ref, doc_ref, gain_ref, wq_ref, wk_ref, wv_ref,
    kv_ref, q_ref, count_ref,
):
    x = masked_rows(series_ref, recon_ref, token_ref)
    factor = lax.rsqrt(jnp.mean(x * x, axis=-1, keepdims=True) + 1e-06)
    normed = (x * factor * gain_ref[...].astype(jnp.float32)).astype(jnp.bfloat16)
    ids = doc_ref[...]
    lane = lax.broadcasted_iota(jnp.int32, (8, 128), 1)
    count = jnp.zeros((8, 128), jnp.int32)
    for d in range(3):
        below = jnp.sum((ids <= d).astype(jnp.float32), axis=1, keepdims=True).astype(jnp.int32)
        count = jnp.where(lane == d, below, count)

    def project(w_ref):
        return jnp.dot(normed, w_ref[...], preferred_element_type=jnp.float32)

    def piece(values, k):
        return values[k * BLK : (k + 1) * BLK]

    key, value = project(wk_ref), project(wv_ref)
    for m in range(HEADS // 2):
        kp, vp = key[:, m * 128 : (m + 1) * 128], value[:, m * 128 : (m + 1) * 128]
        for head, kv in ((2 * m, join(kp, swap(vp))), (2 * m + 1, join(swap(kp), vp))):
            kv = kv.astype(jnp.bfloat16)
            for k in range(N_GROUP):
                kv_ref[packing_ref[k] * TRIPLES + head // PER, head % PER] = piece(kv, k)
    query = project(wq_ref) * SCALE
    for t in range(TRIPLES):
        pair = [query[:, m * 128 : (m + 1) * 128] for m in (3 * t // 2, 3 * t // 2 + 1)]
        if t % 2 == 0:
            first, last = pair[0], pair[1]
        else:
            first, last = join(swap(pair[0]), swap(pair[1])), swap(pair[1])
        first = first.astype(jnp.bfloat16)
        swapped = swap(last)
        for k in range(N_GROUP):
            to = packing_ref[k] * TRIPLES + t
            q_ref[to, 0:BLK] = piece(first, k)
            half = join(last[k * BLK : k * BLK + 16], swapped[k * BLK + 16 : (k + 1) * BLK])
            q_ref[to, BLK:QROWS] = half.astype(jnp.bfloat16)


    count_ref[...] = count


def project(series, recon, token, packing, docs, gain, wq, wk, wv):
    vmem = pl.BlockSpec(memory_space=pltpu.VMEM)
    return pl.pallas_call(
        project_kernel,
        out_shape=(
            jax.ShapeDtypeStruct((N_CTX, PER, BLK, 128), jnp.bfloat16),
            jax.ShapeDtypeStruct((N_CTX, QROWS, 128), jnp.bfloat16),
            jax.ShapeDtypeStruct((8, 128), jnp.int32),
        ),
        in_specs=[pl.BlockSpec(memory_space=pltpu.SMEM)] + [vmem] * 8,
        out_specs=(vmem, vmem, vmem),
        compiler_params=pltpu.CompilerParams(vmem_limit_bytes=48 << 20),
        name="project",
    )(packing, series, recon, token, docs, gain, wq, wk, wv)


def step_z(i):
    return lax.rem(N_Z + (1 - 2 * lax.rem(i + 1, 2)) * ((i + 1) // 2), N_Z)


def spread_kernel(
    kv_ref, q_ref, count_ref, all_ref, qout_ref, total_ref,
    counts, kv_send, kv_recv, q_send, q_recv, c_send, c_recv, self_sem,
    x_send, near_recv, half_recv, pair_recv, t_send, t_recv,
):
    s = lax.axis_index("group")
    c = lax.axis_index("ctx")
    z, y = c // N_Y, lax.rem(c, N_Y)
    partner = s + 1 - 2 * lax.rem(s, 2)
    right, left, across = lax.rem(s + 2, N_GROUP), lax.rem(s + 6, N_GROUP), lax.rem(s + 4, N_GROUP)
    owner = z == s
    bar = pltpu.get_barrier_semaphore()

    def greet(o, carry):
        pl.semaphore_signal(bar, inc=1, device_id=(s, lax.rem(c + o, N_CTX)), device_id_type=MESH)
        return carry

    lax.fori_loop(1, N_CTX, greet, 0)
    for o in range(1, N_GROUP):
        pl.semaphore_signal(bar, inc=1, device_id=(lax.rem(s + o, N_GROUP), c), device_id_type=MESH)
    pl.semaphore_wait(bar, N_CTX - 1 + N_GROUP - 1)

    def rows_of(d):
        return pl.ds(pl.multiple_of(d * BLK, BLK), BLK)

    def send_kv(d, i):
        return pltpu.make_async_remote_copy(
            src_ref=kv_ref.at[d], dst_ref=all_ref.at[:, s, rows_of(c), :],
            send_sem=kv_send, recv_sem=kv_recv.at[i],
            device_id=(s, d), device_id_type=MESH,
        )

    def send_q(d):
        return pltpu.make_async_remote_copy(
            src_ref=q_ref.at[d], dst_ref=qout_ref.at[c], send_sem=q_send, recv_sem=q_recv,
            device_id=(s, d), device_id_type=MESH,
        )

    def send_count(t):
        return pltpu.make_async_remote_copy(
            src_ref=count_ref, dst_ref=counts.at[c], send_sem=c_send.at[t], recv_sem=c_recv,
            device_id=(s, s * N_Y + t), device_id_type=MESH,
        )

    def send_total(o):
        return pltpu.make_async_remote_copy(
            src_ref=total_ref, dst_ref=total_ref, send_sem=t_send.at[o - 1], recv_sem=t_recv,
            device_id=(lax.rem(s + o, N_GROUP), c), device_id_type=MESH,
        )

    def other(i, yy):
        return lax.rem(z + step_z(i), N_Z) * N_Y + lax.rem(y + yy, N_Y)

    own_kv = pltpu.make_async_copy(kv_ref.at[c], all_ref.at[:, s, rows_of(c), :], self_sem.at[0])
    own_q = pltpu.make_async_copy(q_ref.at[c], qout_ref.at[c], self_sem.at[1])
    own_kv.start()
    for yy in range(1, N_Y):
        send_kv(other(0, yy), 0).start()

    def start_plane(i, carry):
        for yy in range(N_Y):
            send_kv(other(i, yy), i).start()
        return carry

    lax.fori_loop(1, 3, start_plane, 0)
    for t in range(N_Y):
        @pl.when(s * N_Y + t != c)
        def _():
            send_count(t).start()

    lax.fori_loop(3, N_Z, start_plane, 0)
    own_q.start()

    def start_q(i, carry):
        for yy in range(N_Y):
            send_q(other(i, yy)).start()
        return carry

    for yy in range(1, N_Y):
        send_q(other(0, yy)).start()
    lax.fori_loop(1, N_Z, start_q, 0)

    def plane(i):
        return lax.rem(z + N_Z - step_z(i), N_Z)

    def hop(slot, i, to, kind, recv, half=None):
        first, size = plane(i) * 128, 128
        if half is not None:
            first, size = first + half * 64, 64
        part = all_ref.at[:, slot, pl.ds(pl.multiple_of(first, 64), size), :]
        return pltpu.make_async_remote_copy(
            src_ref=part, dst_ref=part, send_sem=x_send.at[kind], recv_sem=recv,
            device_id=(to, c), device_id_type=MESH,
        )

    def whole(slot, kind, recv, half=None):
        part = all_ref.at[:, slot, pl.ds(0, ROWS if half is None else ROWS // 2), :]
        return pltpu.make_async_remote_copy(
            src_ref=part, dst_ref=part, send_sem=x_send.at[kind], recv_sem=recv,
            device_id=(partner, c), device_id_type=MESH,
        )

    def send_own(i):
        hop(s, i, right, 0, near_recv.at[0, i]).start()
        hop(s, i, left, 1, near_recv.at[1, i]).start()
        hop(s, i, partner, 2, pair_recv.at[0]).start()

    def send_near(i):
        hop(left, i, left, 0, near_recv.at[0, i]).wait_recv()
        hop(left, i, right, 3, half_recv.at[0, i], half=0).start()
        hop(left, i, partner, 5, pair_recv.at[1]).start()
        hop(right, i, right, 1, near_recv.at[1, i]).wait_recv()
        hop(right, i, left, 4, half_recv.at[1, i], half=1).start()
        hop(right, i, partner, 6, pair_recv.at[2]).start()

    def send_across(i):
        hop(across, i, left, 3, half_recv.at[0, i], half=0).wait_recv()
        hop(across, i, right, 4, half_recv.at[1, i], half=1).wait_recv()
        hop(across, i, partner, 7, pair_recv.at[3]).start()

    def arrive_plane(i):
        part = all_ref.at[:, s, pl.ds(pl.multiple_of(plane(i) * 128, 128), 128), :]
        pltpu.make_async_remote_copy(
            src_ref=part, dst_ref=part, send_sem=kv_send, recv_sem=kv_recv.at[i],
            device_id=(partner, c), device_id_type=MESH,
        ).wait_recv()

    own_kv.wait()
    three = all_ref.at[:, s, pl.ds(pl.multiple_of(z * 128, 128), 96), :]
    pltpu.make_async_remote_copy(
        src_ref=three, dst_ref=three, send_sem=kv_send, recv_sem=kv_recv.at[0],
        device_id=(partner, c), device_id_type=MESH,
    ).wait_recv()
    send_own(0)
    arrive_plane(1)
    send_own(1)
    send_near(0)

    def step(i, carry):
        arrive_plane(i)
        send_own(i)
        send_near(i - 1)
        send_across(i - 2)
        return carry

    lax.fori_loop(2, 5, step, 0)

    @pl.when(owner)
    def _():
        counts[c] = count_ref[...]
        rest = counts.at[pl.ds(0, N_CTX - 1)]
        pltpu.make_async_remote_copy(
            src_ref=rest, dst_ref=rest, send_sem=c_send.at[0], recv_sem=c_recv,
            device_id=(partner, c), device_id_type=MESH,
        ).wait_recv()
        total_ref[...] = jnp.sum(counts[...], axis=0)
        for o in range(1, N_GROUP):
            send_total(o).start()

    lax.fori_loop(5, N_Z, step, 0)
    send_near(N_Z - 1)
    send_across(N_Z - 2)
    send_across(N_Z - 1)

    for t in range(N_Y):
        @pl.when(s * N_Y + t != c)
        def _():
            send_count(t).wait_send()

    @pl.when(owner)
    def _():
        for o in range(1, N_GROUP):
            send_total(o).wait_send()

    @pl.when(jnp.logical_not(owner))
    def _():
        send_total(1).wait_recv()

    own_q.wait()
    rest = pltpu.make_async_remote_copy(
        src_ref=q_ref.at[pl.ds(0, N_CTX - 1)], dst_ref=qout_ref.at[pl.ds(0, N_CTX - 1)],
        send_sem=q_send, recv_sem=q_recv, device_id=(partner, c), device_id_type=MESH,
    )
    rest.wait_recv()
    rest.wait_send()
    sent = kv_ref.at[pl.ds(0, N_CTX - 1)]
    pltpu.make_async_remote_copy(
        src_ref=sent, dst_ref=sent, send_sem=kv_send, recv_sem=kv_recv.at[0],
        device_id=(partner, c), device_id_type=MESH,
    ).wait_send()
    for kind, slot in enumerate((s, s, s, left, right, left, right, across)):
        whole(slot, kind, t_recv, half=0 if kind in (3, 4) else None).wait_send()
    slots = (partner, lax.rem(partner + 6, N_GROUP), lax.rem(partner + 2, N_GROUP), lax.rem(partner + 4, N_GROUP))
    for n, slot in enumerate(slots):
        whole(slot, 2, pair_recv.at[n]).wait_recv()


def spread(kv, q, count):
    anywhere = pl.BlockSpec(memory_space=pl.ANY)
    vmem = pl.BlockSpec(memory_space=pltpu.VMEM)
    dma = pltpu.SemaphoreType.DMA
    return pl.pallas_call(
        spread_kernel,
        out_shape=(
            jax.ShapeDtypeStruct((PER, N_GROUP, ROWS, 128), jnp.bfloat16),
            jax.ShapeDtypeStruct((N_CTX, QROWS, 128), jnp.bfloat16),
            jax.ShapeDtypeStruct((8, 128), jnp.int32),
        ),
        in_specs=[anywhere, anywhere, vmem],
        out_specs=(anywhere, anywhere, vmem),
        scratch_shapes=[
            pltpu.VMEM((N_CTX, 8, 128), jnp.int32),
            dma(()), dma((N_Z,)), dma(()), dma(()), dma((N_Y,)), dma(()), dma((2,)),
            dma((8,)), dma((2, N_Z)), dma((2, N_Z)), dma((4,)), dma((N_GROUP - 1,)), dma(()),
        ],
        compiler_params=pltpu.CompilerParams(collective_id=0, has_side_effects=True),
        name="spread",
    )(kv, q, count)


def attend_kernel(total_ref, q_ref, kv_ref, out_ref, kv, qt, k1, vt, acc, top, sem):
    s = lax.axis_index("group")
    copies = [pltpu.make_async_copy(kv_ref.at[h], kv.at[h], sem.at[h]) for h in range(PER)]
    for copy in copies:
        copy.start()
    starts = [total_ref[0, d] for d in range(3)]
    first, last = [jnp.int32(0)] + starts, starts + [jnp.int32(N_CTX * 256)]

    def edges(index):
        lo, hi = jnp.full(index.shape, N_CTX * 256), jnp.zeros(index.shape, jnp.int32)
        for d in range(DOCS):
            lo = jnp.where(index == HD + d, first[d], lo)
            hi = jnp.where(index == HD + d, last[d], hi)
        return lo, hi

    col = lax.broadcasted_iota(jnp.int32, (1, ROWS), 1)
    pos = (col // BLK) * 256 + s * BLK + col % BLK
    row = lax.broadcasted_iota(jnp.int32, (HD, 1), 0) + HD
    lo, hi = edges(row)
    own = (pos >= lo) & (pos < hi)
    far = jnp.where(own | (row >= HD + DOCS), 0.0, NEGATIVE)

    a = q_ref[:, 0:BLK, :].reshape(ROWS, 128).astype(jnp.float32).T
    b = q_ref[:, BLK:QROWS, :].astype(jnp.float32)
    b = jnp.concatenate([b, swap(b.reshape(ROWS // 2, 128)).reshape(N_CTX, 16, 128)], axis=1)
    b = b.reshape(ROWS, 128).T
    q_top = []
    for h, part in enumerate((a[0:HD], a[HD:128], b[0:HD])):
        q_top.append(jnp.max(jnp.sum(part * part, axis=0, keepdims=True)))
        qt[h] = jnp.concatenate([part, far], axis=0).astype(jnp.bfloat16)

    r = lax.broadcasted_iota(jnp.int32, (ROWS, 128), 0)
    base = (r // BLK) * 256 + r % BLK
    lo, hi = edges(lax.broadcasted_iota(jnp.int32, (1, 128), 1))
    keys_n = KC * 256
    low = low_half((ROWS, 128))
    vt[:, :, 0:16, :] = jnp.ones((PER, N_CTX // KC, 16, keys_n), jnp.bfloat16)
    small = None
    for h in range(PER):
        copies[h].wait()
        for n in range(N_GROUP):
            both = kv[h, n]
            if h == 0:
                own = (base >= lo - n * BLK) & (base < hi - n * BLK)
                mark = jnp.where(own, 1.0, 0.0).astype(jnp.bfloat16)
            else:
                mark = k1[0, n]
            k1[h, n] = jnp.where(low, both, mark)
        norms = jnp.zeros((1, keys_n), jnp.float32)
        for kb in range(N_CTX // KC):
            block = kv[h, :, kb * KC * BLK : (kb + 1) * KC * BLK, :].reshape(keys_n, 128).T
            vt[h, kb, 16:80, :] = block[HD:128]
            keys = block[0:HD].astype(jnp.float32)
            norms = jnp.maximum(norms, jnp.sum(keys * keys, axis=0, keepdims=True))
        fits = q_top[h] * jnp.max(norms) * 1.05 <= BOUND * BOUND
        small = fits if small is None else small & fits

    span = TQ // BLK * 256
    blocks = TQ // BLK

    def tile(t, carry):
        p0 = t * span
        p1 = p0 + span - 1
        lo, hi = jnp.int32(0), jnp.int32(N_CTX * 256)
        for st in starts:
            lo = jnp.maximum(lo, jnp.where(st <= p0, st, 0))
            hi = jnp.minimum(hi, jnp.where(st > p1, st, N_CTX * 256))
        begin, end = lo // keys_n, (hi + keys_n - 1) // keys_n
        cols = pl.ds(pl.multiple_of(t * TQ, TQ), TQ)

        def scores(h, kb):
            rows = pl.ds(pl.multiple_of(kb * KC * BLK, KC * BLK), KC * BLK)
            keys = k1[h, :, rows, :].reshape(keys_n, 128)
            return jnp.dot(keys, qt[h, :, cols], preferred_element_type=jnp.float32)

        def summed(h, kb, p):
            return jnp.dot(vt[h, kb], p, preferred_element_type=jnp.float32)

        acc[...] = jnp.zeros_like(acc)

        @pl.when(small)
        def _():
            def body(kb, carry):
                weights = [scores(h, kb) for h in range(PER)]
                weights = [jnp.exp2(w).astype(jnp.bfloat16) for w in weights]
                sums = [summed(h, kb, weights[h]) for h in range(PER)]
                for h in range(PER):
                    acc[h] += sums[h]
                return carry

            lax.fori_loop(begin, end, body, 0)

        @pl.when(jnp.logical_not(small))
        def _():
            top[...] = jnp.full_like(top, NEGATIVE)

            def body(kb, carry):
                all_scores = [scores(h, kb) for h in range(PER)]
                for h, sc in enumerate(all_scores):
                    old = top[h]
                    new = jnp.maximum(old, jnp.max(sc, axis=0, keepdims=True))
                    top[h] = new
                    weights = jnp.exp2(sc - new).astype(jnp.bfloat16)
                    acc[h] = acc[h] * jnp.exp2(old - new) + summed(h, kb, weights)
                return carry

            lax.fori_loop(begin, end, body, 0)

        def attended(h):
            return acc[h, 16:80, :] / acc[h, 0:1, :]

        here = pl.ds(t * blocks, blocks)
        o = jnp.concatenate([attended(0), attended(1)], axis=0).T
        out_ref[here, 0:BLK] = o.astype(jnp.bfloat16).reshape(blocks, BLK, 128)
        o = attended(2)
        o = jnp.concatenate([o, o], axis=0).T.reshape(blocks, BLK, 128)
        one, two = o[:, 0:16].reshape(TQ // 2, 128), o[:, 16:32].reshape(TQ // 2, 128)
        out_ref[here, BLK:QROWS] = join(one, two).astype(jnp.bfloat16).reshape(blocks, 16, 128)
        return carry

    lax.fori_loop(0, ROWS // TQ, tile, 0)


def attend(total, q, kv):
    vmem = pl.BlockSpec(memory_space=pltpu.VMEM)
    wide = pltpu.VMEM((PER, N_GROUP, ROWS, 128), jnp.bfloat16)
    return pl.pallas_call(
        attend_kernel,
        out_shape=jax.ShapeDtypeStruct((N_CTX, QROWS, 128), jnp.bfloat16),
        in_specs=[pl.BlockSpec(memory_space=pltpu.SMEM), vmem, pl.BlockSpec(memory_space=pl.ANY)],
        out_specs=vmem,
        scratch_shapes=[
            wide,
            pltpu.VMEM((PER, 128, ROWS), jnp.bfloat16),
            wide,
            pltpu.VMEM((PER, N_CTX // KC, 80, KC * 256), jnp.bfloat16),
            pltpu.VMEM((PER, 80, TQ), jnp.float32),
            pltpu.VMEM((PER, 1, TQ), jnp.float32),
            pltpu.SemaphoreType.DMA((PER,)),
        ],
        compiler_params=pltpu.CompilerParams(vmem_limit_bytes=56 << 20),
        name="attend",
    )(total, q, kv)


def finish_kernel(packing_ref, att_ref, series_ref, recon_ref, token_ref, w_ref, out_ref, lhs, w2):
    order = [PER * t + n for t in range(TRIPLES) for n in range(2)] + [2, 5, 8, 11]
    for n, head in enumerate(order):
        w2[n * HD : (n + 1) * HD, :] = w_ref[head * HD : (head + 1) * HD, :]
    for k in range(N_GROUP):
        g = packing_ref[k]
        rows = slice(k * BLK, (k + 1) * BLK)
        for t in range(TRIPLES):
            lhs[rows, t * 128 : (t + 1) * 128] = att_ref[g * TRIPLES + t, 0:BLK]
        for n in range(2):
            a = att_ref[g * TRIPLES + 2 * n, BLK:QROWS].astype(jnp.float32)
            b = att_ref[g * TRIPLES + 2 * n + 1, BLK:QROWS].astype(jnp.float32)
            cols = slice((TRIPLES + n) * 128, (TRIPLES + n + 1) * 128)
            lhs[k * BLK : k * BLK + 16, cols] = join(a, swap(b)).astype(jnp.bfloat16)
            lhs[k * BLK + 16 : (k + 1) * BLK, cols] = join(swap(a), b).astype(jnp.bfloat16)
    mixed = jnp.dot(lhs[...], w2[...], preferred_element_type=jnp.float32)
    out_ref[...] = (masked_rows(series_ref, recon_ref, token_ref) + mixed).astype(jnp.bfloat16)


def finish(packing, att, series, recon, token, w_out):
    vmem = pl.BlockSpec(memory_space=pltpu.VMEM)
    return pl.pallas_call(
        finish_kernel,
        out_shape=jax.ShapeDtypeStruct(series.shape, jnp.bfloat16),
        in_specs=[pl.BlockSpec(memory_space=pltpu.SMEM)] + [vmem] * 5,
        out_specs=vmem,
        scratch_shapes=[pltpu.VMEM((N_GROUP * BLK, D), jnp.bfloat16), pltpu.VMEM((D, D), jnp.bfloat16)],
        compiler_params=pltpu.CompilerParams(vmem_limit_bytes=48 << 20),
        name="finish",
    )(packing, att, series, recon, token, w_out)


def on_device(
    series, recon_mask, mask_token, packing_list, doc_ids, norm_gain, w_query, w_key, w_value, w_out
):
    recon = recon_mask.reshape(-1, 1)
    token = mask_token.reshape(1, -1)
    kv, q, count = project(
        series, recon, token, packing_list, doc_ids, norm_gain.reshape(1, -1), w_query, w_key, w_value
    )
    all_kv, q_rows, total = spread(kv, q, count)
    att = attend(total, q_rows, all_kv)
    back = lax.all_to_all(att, "ctx", split_axis=0, concat_axis=0, tiled=True)
    return finish(packing_list, back, series, recon, token, w_out)


def solution(mesh):
    split = P(("group", "ctx"))
    in_specs = (
        P(("group", "ctx"), None), split, P(), split, P("group", "ctx"), P(), P(), P(), P(), P(),
    )
    return jax.shard_map(
        on_device, mesh=mesh, in_specs=in_specs, out_specs=P(("group", "ctx"), None), check_vma=False
    )
```

time: 151 us -> 129 us (0.85)
  Pallas kernels: 122 us -> 99.1 us
    pallas_call x1, Pallas kernels: 58.8 us -> 43.4 us  [attend(): pl.pallas_call(attend_kernel, out_shape=jax.ShapeDtypeStruct((N_CTX, QROW...]
    pallas_call x1, Pallas kernels: 59 us -> 51.8 us  [spread(): pl.pallas_call(spread_kernel, out_shape=(jax.ShapeDtypeStruct((PER, N_GRO...]
where the time goes in v2:
time: 129 us; the launch traced here: 128 us
  Pallas kernels  99.1 us (77%)
  blocking collectives  18.3 us (14%)
  local copies, waits for them, and re-layouts  10.5 us (8%)
    pallas_call x1, Pallas kernels, spread(): pl.pallas_call(spread_kernel, out_shape=(jax.ShapeDtypeStruct((PER, N_GRO...  51.8 us
    pallas_call x1, Pallas kernels, attend(): pl.pallas_call(attend_kernel, out_shape=jax.ShapeDtypeStruct((N_CTX, QROW...  43.4 us
    all_to_all x1, blocking collectives, on_device(): back = lax.all_to_all(att, 'ctx', split_axis=0, concat_axis=0, tiled=True)  18.3 us
    unnamed x24, local copies, waits for them, and re-layouts  8.38 us

profile of v2, /device:TPU:1, one launch (start us, length us, event | category | flops | bytes accessed | tf_op | source)
XLA Modules:
  0.0 128.0 jit_solution(9282491753950527165)
XLA Ops:
  0.0 0.7 reshape.10.token_ref
  0.7 0.7 reshape.11.gain_ref
  1.4 0.8 copy.11.recon_ref
  2.2 0.0 copy-start
  2.2 1.0 copy-done
  3.2 0.0 copy-start.3
  3.2 1.3 copy-done.3
  4.5 0.0 copy-start.4
  4.5 1.3 copy-done.4
  5.7 0.0 copy-start.5
  5.7 1.3 copy-done.5
  7.0 0.0 copy-start.9
  7.0 0.7 copy-done.9
  7.7 0.0 copy-start.11
  7.7 0.7 copy-done.11
  8.3 2.1 %project.1 = (bf16[32,3,32,128]{3,2,1,0:T(8,128)(2,1)S(1)}, bf16[32,48,128]{2,1,0:T(8,128)(2,1)S(1)}, s32[8,128]{1,0:T(8,128)S(1)}) custom-call(s32[8]{0:T(128)S(1)} %copy-done.9, bf16[256,768]{1,0:T(8,128)(2,1)S(1)} %copy-done, s32[256,1]{1,0:T(8,128)S(1)} %copy.11.recon_ref, bf16[1,768]{1,0:T(2,128)(2,1)S(1)} %reshape.10.token_ref, ...), custom_call_target="tpu_custom_call" | custom-call | tf_op jit(solution)/shard_map/project/pallas_call | solution.py:98
  10.4 0.0 copy-start.6
  10.4 0.9 copy-done.6
  11.3 0.0 copy-start.7
  11.3 0.7 copy-done.7
  12.1 0.0 copy-start.8
  12.1 0.6 copy-done.8
  12.7 51.8 %spread.1 = (bf16[3,8,1024,128]{3,2,1,0:T(8,128)(2,1)}, bf16[32,48,128]{2,1,0:T(8,128)(2,1)}, s32[8,128]{1,0:T(8,128)}) custom-call(bf16[32,3,32,128]{3,2,1,0:T(8,128)(2,1)} %copy-done.6, bf16[32,48,128]{2,1,0:T(8,128)(2,1)} %copy-done.7, s32[8,128]{1,0:T(8,128)} %copy-done.8), custom_call_target="tpu_custom_call" | custom-call | tf_op jit(solution)/shard_map/spread/pallas_call | solution.py:317
  64.4 0.0 copy-start.1
  64.4 0.0 copy-start.2
  64.5 0.0 copy-start.10
  64.5 43.4 %attend.1 = bf16[32,48,128]{2,1,0:T(8,128)(2,1)} custom-call(s32[8,128]{1,0:T(8,128)} %get-tuple-element.14.total_ref, bf16[32,48,128]{2,1,0:T(8,128)(2,1)} %get-tuple-element.15.q_ref, bf16[3,8,1024,128]{3,2,1,0:T(8,128)(2,1)} %get-tuple-element.16.kv_ref), custom_call_target="tpu_custom_call" | custom-call | tf_op jit(solution)/shard_map/attend/pallas_call | solution.py:462
  107.9 18.3 %all_to_all.5.att_ref = bf16[32,48,128]{2,1,0:T(8,128)(2,1)S(1)} all-to-all(bf16[32,48,128]{2,1,0:T(8,128)(2,1)} %attend.1), channel_id=1, replica_groups=mesh['group'=8,'ctx'=32] {'ctx'}, dimensions={0} | all-to-all | bytes 786432 | tf_op jit(solution)/shard_map/all_to_all | solution.py:523
  126.2 0.0 copy-done.1
  126.2 0.0 copy-done.2
  126.2 0.0 copy-done.10
  126.2 1.8 %finish.1 = bf16[256,768]{1,0:T(8,128)(2,1)} custom-call(s32[8]{0:T(128)S(1)} %copy-done.10, bf16[32,48,128]{2,1,0:T(8,128)(2,1)S(1)} %all_to_all.5.att_ref, bf16[256,768]{1,0:T(8,128)(2,1)S(1)} %copy-done.1, s32[256,1]{1,0:T(8,128)S(1)} %copy.11.recon_ref, bf16[1,768]{1,0:T(2,128)(2,1)S(1)} %reshape.10.token_ref, bf16[768,768]{1,0:T(8,128)(2,1)S(1)} %copy-done.2), custom_call_target="tpu_custom_call" | custom-call | tf_op jit(solution)/shard_map/finish/pallas_call | solution.py:502
Async XLA Ops:
  2.2 1.0 copy-start
  3.2 1.3 copy-start.3
  4.5 1.3 copy-start.4
  5.7 1.3 copy-start.5
  7.0 0.7 copy-start.9
  7.7 0.7 copy-start.11
  10.4 0.9 copy-start.6
  11.3 0.7 copy-start.7
  12.1 0.6 copy-start.8
  64.4 61.8 %copy-start.1 = (bf16[256,768]{1,0:T(8,128)(2,1)S(1)}, bf16[256,768]{1,0:T(8,128)(2,1)}, u32[]{:S(2)}) copy-start(bf16[256,768]{1,0:T(8,128)(2,1)} %series_ref.3) | copy-start | bytes 1179652
  64.4 61.8 %copy-start.2 = (bf16[768,768]{1,0:T(8,128)(2,1)S(1)}, bf16[768,768]{1,0:T(8,128)(2,1)}, u32[]{:S(2)}) copy-start(bf16[768,768]{1,0:T(8,128)(2,1)} %w_ref.1) | copy-start | bytes 3538948
  64.5 61.8 %copy-start.10 = (s32[8]{0:T(128)S(1)}, s32[8]{0:T(128)}, u32[]{:S(2)}) copy-start(s32[8]{0:T(128)} %packing_ref.3) | copy-start | bytes 100

commit v3 on v2

--- a/solution.py
+++ b/solution.py
@@ -41,40 +41,53 @@
     return jnp.where(low_half(a.shape), a, b)
 
 
-def masked_rows(series_ref, recon_ref, token_ref):
-    return jnp.where(
-        recon_ref[...] == 1, token_ref[...].astype(jnp.float32), series_ref[...].astype(jnp.float32)
-    )
-
-
-def project_kernel(
-    packing_ref, series_ref, recon_ref, token_ref, doc_ref, gain_ref, wq_ref, wk_ref, wv_ref,
-    kv_ref, q_ref, count_ref,
-):
-    x = masked_rows(series_ref, recon_ref, token_ref)
+def row_mask(recon_ref):
+    flags = recon_ref[...].astype(jnp.float32)
+    return jnp.broadcast_to(flags, (128, flags.shape[1])).T
+
+
+def masked_rows(rows, flags, token_ref):
+    flags = jnp.concatenate([flags] * (D // 128), axis=1)
+    return jnp.where(flags == 1.0, token_ref[...].astype(jnp.float32), rows.astype(jnp.float32))
+
+
+def normed_rows(packing_ref, series_ref, recon_ref, token_ref, gain_ref, flags):
+    flags[...] = row_mask(recon_ref).reshape(N_GROUP, BLK, 128)
+    pieces = []
+    for g in range(N_GROUP):
+        at = jnp.int32(0)
+        for k in range(1, N_GROUP):
+            at = jnp.where(packing_ref[k] == g, k, at)
+        pieces.append(masked_rows(series_ref[at], flags[at], token_ref))
+    x = jnp.concatenate(pieces, axis=0)
     factor = lax.rsqrt(jnp.mean(x * x, axis=-1, keepdims=True) + 1e-06)
-    normed = (x * factor * gain_ref[...].astype(jnp.float32)).astype(jnp.bfloat16)
+    return (x * factor * gain_ref[...].astype(jnp.float32)).astype(jnp.bfloat16)
+
+
+def document_counts(doc_ref):
     ids = doc_ref[...]
     lane = lax.broadcasted_iota(jnp.int32, (8, 128), 1)
     count = jnp.zeros((8, 128), jnp.int32)
-    for d in range(3):
+    for d in range(DOCS - 1):
         below = jnp.sum((ids <= d).astype(jnp.float32), axis=1, keepdims=True).astype(jnp.int32)
         count = jnp.where(lane == d, below, count)
-
-    def project(w_ref):
-        return jnp.dot(normed, w_ref[...], preferred_element_type=jnp.float32)
-
-    def piece(values, k):
-        return values[k * BLK : (k + 1) * BLK]
-
-    key, value = project(wk_ref), project(wv_ref)
+    return count
+
+
+def piece(values, g):
+    return values[g * BLK : (g + 1) * BLK]
+
+
+def pack_keys(kv_ref, key, value):
     for m in range(HEADS // 2):
         kp, vp = key[:, m * 128 : (m + 1) * 128], value[:, m * 128 : (m + 1) * 128]
         for head, kv in ((2 * m, join(kp, swap(vp))), (2 * m + 1, join(swap(kp), vp))):
             kv = kv.astype(jnp.bfloat16)
-            for k in range(N_GROUP):
-                kv_ref[packing_ref[k] * TRIPLES + head // PER, head % PER] = piece(kv, k)
-    query = project(wq_ref) * SCALE
+            for g in range(N_GROUP):
+                kv_ref[g * TRIPLES + head // PER, head % PER] = piece(kv, g)
+
+
+def pack_queries(q_ref, query):
     for t in range(TRIPLES):
         pair = [query[:, m * 128 : (m + 1) * 128] for m in (3 * t // 2, 3 * t // 2 + 1)]
         if t % 2 == 0:
@@ -83,30 +96,11 @@
             first, last = join(swap(pair[0]), swap(pair[1])), swap(pair[1])
         first = first.astype(jnp.bfloat16)
         swapped = swap(last)
-        for k in range(N_GROUP):
-            to = packing_ref[k] * TRIPLES + t
-            q_ref[to, 0:BLK] = piece(first, k)
-            half = join(last[k * BLK : k * BLK + 16], swapped[k * BLK + 16 : (k + 1) * BLK])
+        for g in range(N_GROUP):
+            to = g * TRIPLES + t
+            q_ref[to, 0:BLK] = piece(first, g)
+            half = join(last[g * BLK : g * BLK + 16], swapped[g * BLK + 16 : (g + 1) * BLK])
             q_ref[to, BLK:QROWS] = half.astype(jnp.bfloat16)
-
-
-    count_ref[...] = count
-
-
-def project(series, recon, token, packing, docs, gain, wq, wk, wv):
-    vmem = pl.BlockSpec(memory_space=pltpu.VMEM)
-    return pl.pallas_call(
-        project_kernel,
-        out_shape=(
-            jax.ShapeDtypeStruct((N_CTX, PER, BLK, 128), jnp.bfloat16),
-            jax.ShapeDtypeStruct((N_CTX, QROWS, 128), jnp.bfloat16),
-            jax.ShapeDtypeStruct((8, 128), jnp.int32),
-        ),
-        in_specs=[pl.BlockSpec(memory_space=pltpu.SMEM)] + [vmem] * 8,
-        out_specs=(vmem, vmem, vmem),
-        compiler_params=pltpu.CompilerParams(vmem_limit_bytes=48 << 20),
-        name="project",
-    )(packing, series, recon, token, docs, gain, wq, wk, wv)
 
 
 def step_z(i):
@@ -114,8 +108,9 @@
 
 
 def spread_kernel(
-    kv_ref, q_ref, count_ref, all_ref, qout_ref, total_ref,
-    counts, kv_send, kv_recv, q_send, q_recv, c_send, c_recv, self_sem,
+    packing_ref, series_ref, recon_ref, token_ref, doc_ref, gain_ref, wq_ref, wk_ref, wv_ref,
+    all_ref, qout_ref, total_ref,
+    kv_ref, q_ref, count_ref, flags, wq, wk, wv, w_sem, counts, kv_send, kv_recv, q_send, q_recv, c_send, c_recv, self_sem,
     x_send, near_recv, half_recv, pair_recv, t_send, t_recv,
 ):
     s = lax.axis_index("group")
@@ -133,6 +128,20 @@
     lax.fori_loop(1, N_CTX, greet, 0)
     for o in range(1, N_GROUP):
         pl.semaphore_signal(bar, inc=1, device_id=(lax.rem(s + o, N_GROUP), c), device_id_type=MESH)
+    loads = [
+        pltpu.make_async_copy(src, dst, w_sem.at[n])
+        for n, (src, dst) in enumerate(((wk_ref, wk), (wv_ref, wv), (wq_ref, wq)))
+    ]
+    for load in loads:
+        load.start()
+    count_ref[...] = document_counts(doc_ref)
+    normed = normed_rows(packing_ref, series_ref, recon_ref, token_ref, gain_ref, flags)
+
+    def project(n, w):
+        loads[n].wait()
+        return jnp.dot(normed, w[...], preferred_element_type=jnp.float32)
+
+    pack_keys(kv_ref, project(0, wk), project(1, wv))
     pl.semaphore_wait(bar, N_CTX - 1 + N_GROUP - 1)
 
     def rows_of(d):
@@ -184,6 +193,7 @@
             send_count(t).start()
 
     lax.fori_loop(3, N_Z, start_plane, 0)
+    pack_queries(q_ref, project(2, wq) * SCALE)
     own_q.start()
 
     def start_q(i, carry):
@@ -310,10 +320,11 @@
         whole(slot, 2, pair_recv.at[n]).wait_recv()
 
 
-def spread(kv, q, count):
-    anywhere = pl.BlockSpec(memory_space=pl.ANY)
+def spread(packing, series, recon, token, docs, gain, w_query, w_key, w_value):
+    anywhere = pl.BlockSpec(memory_space=pltpu.HBM)
     vmem = pl.BlockSpec(memory_space=pltpu.VMEM)
     dma = pltpu.SemaphoreType.DMA
+    weight = pltpu.VMEM((D, D), jnp.bfloat16)
     return pl.pallas_call(
         spread_kernel,
         out_shape=(
@@ -321,23 +332,28 @@
             jax.ShapeDtypeStruct((N_CTX, QROWS, 128), jnp.bfloat16),
             jax.ShapeDtypeStruct((8, 128), jnp.int32),
         ),
-        in_specs=[anywhere, anywhere, vmem],
+        in_specs=[pl.BlockSpec(memory_space=pltpu.SMEM)] + [vmem] * 5 + [anywhere] * 3,
         out_specs=(anywhere, anywhere, vmem),
         scratch_shapes=[
+            pltpu.VMEM((N_CTX, PER, BLK, 128), jnp.bfloat16),
+            pltpu.VMEM((N_CTX, QROWS, 128), jnp.bfloat16),
+            pltpu.VMEM((8, 128), jnp.int32),
+            pltpu.VMEM((N_GROUP, BLK, 128), jnp.float32),
+            weight, weight, weight,
+            dma((3,)),
             pltpu.VMEM((N_CTX, 8, 128), jnp.int32),
             dma(()), dma((N_Z,)), dma(()), dma(()), dma((N_Y,)), dma(()), dma((2,)),
             dma((8,)), dma((2, N_Z)), dma((2, N_Z)), dma((4,)), dma((N_GROUP - 1,)), dma(()),
         ],
-        compiler_params=pltpu.CompilerParams(collective_id=0, has_side_effects=True),
+        compiler_params=pltpu.CompilerParams(
+            collective_id=0, has_side_effects=True, vmem_limit_bytes=32 << 20
+        ),
         name="spread",
-    )(kv, q, count)
-
-
-def attend_kernel(total_ref, q_ref, kv_ref, out_ref, kv, qt, k1, vt, acc, top, sem):
+    )(packing, series, recon, token, docs, gain, w_query, w_key, w_value)
+
+
+def attend_kernel(total_ref, q_ref, kv, out_ref, qt, k1, vt, acc, top):
     s = lax.axis_index("group")
-    copies = [pltpu.make_async_copy(kv_ref.at[h], kv.at[h], sem.at[h]) for h in range(PER)]
-    for copy in copies:
-        copy.start()
     starts = [total_ref[0, d] for d in range(3)]
     first, last = [jnp.int32(0)] + starts, starts + [jnp.int32(N_CTX * 256)]
 
@@ -372,7 +388,6 @@
     vt[:, :, 0:16, :] = jnp.ones((PER, N_CTX // KC, 16, keys_n), jnp.bfloat16)
     small = None
     for h in range(PER):
-        copies[h].wait()
         for n in range(N_GROUP):
             both = kv[h, n]
             if h == 0:
@@ -462,18 +477,16 @@
     return pl.pallas_call(
         attend_kernel,
         out_shape=jax.ShapeDtypeStruct((N_CTX, QROWS, 128), jnp.bfloat16),
-        in_specs=[pl.BlockSpec(memory_space=pltpu.SMEM), vmem, pl.BlockSpec(memory_space=pl.ANY)],
+        in_specs=[pl.BlockSpec(memory_space=pltpu.SMEM), vmem, vmem],
         out_specs=vmem,
         scratch_shapes=[
-            wide,
             pltpu.VMEM((PER, 128, ROWS), jnp.bfloat16),
             wide,
             pltpu.VMEM((PER, N_CTX // KC, 80, KC * 256), jnp.bfloat16),
             pltpu.VMEM((PER, 80, TQ), jnp.float32),
             pltpu.VMEM((PER, 1, TQ), jnp.float32),
-            pltpu.SemaphoreType.DMA((PER,)),
         ],
-        compiler_params=pltpu.CompilerParams(vmem_limit_bytes=56 << 20),
+        compiler_params=pltpu.CompilerParams(vmem_limit_bytes=40 << 20),
         name="attend",
     )(total, q, kv)
 
@@ -494,7 +507,8 @@
             lhs[k * BLK : k * BLK + 16, cols] = join(a, swap(b)).astype(jnp.bfloat16)
             lhs[k * BLK + 16 : (k + 1) * BLK, cols] = join(swap(a), b).astype(jnp.bfloat16)
     mixed = jnp.dot(lhs[...], w2[...], preferred_element_type=jnp.float32)
-    out_ref[...] = (masked_rows(series_ref, recon_ref, token_ref) + mixed).astype(jnp.bfloat16)
+    rows = masked_rows(series_ref[...], row_mask(recon_ref), token_ref)
+    out_ref[...] = (rows + mixed).astype(jnp.bfloat16)
 
 
 def finish(packing, att, series, recon, token, w_out):
@@ -513,12 +527,12 @@
 def on_device(
     series, recon_mask, mask_token, packing_list, doc_ids, norm_gain, w_query, w_key, w_value, w_out
 ):
-    recon = recon_mask.reshape(-1, 1)
+    recon = recon_mask.reshape(1, -1)
     token = mask_token.reshape(1, -1)
-    kv, q, count = project(
-        series, recon, token, packing_list, doc_ids, norm_gain.reshape(1, -1), w_query, w_key, w_value
+    all_kv, q_rows, total = spread(
+        packing_list, series.reshape(N_GROUP, BLK, D), recon, token, doc_ids, norm_gain.reshape(1, -1),
+        *(pltpu.with_memory_space_constraint(w, pltpu.HBM) for w in (w_query, w_key, w_value)),
     )
-    all_kv, q_rows, total = spread(kv, q, count)
     att = attend(total, q_rows, all_kv)
     back = lax.all_to_all(att, "ctx", split_axis=0, concat_axis=0, tiled=True)
     return finish(packing_list, back, series, recon, token, w_out)

time: 129 us -> 116 us (0.90)
  Pallas kernels: 99.1 us -> 80.1 us
  blocking collectives: 18.3 us -> 30.3 us
  local copies, waits for them, and re-layouts: 10.5 us -> 4.4 us
    pallas_call x1, Pallas kernels: 43.4 us -> 29.7 us  [attend(): pl.pallas_call(attend_kernel, out_shape=jax.ShapeDtypeStruct((N_CTX, QROW...]
    all_to_all x1, blocking collectives: 18.3 us -> 30.3 us  [on_device(): back = lax.all_to_all(att, 'ctx', split_axis=0, concat_axis=0, tiled=True)]
    unnamed x24 -> x16, local copies, waits for them, and re-layouts: 8.38 us -> 3.03 us
    pallas_call x1, Pallas kernels: 51.8 us -> 48.6 us  [spread(): pl.pallas_call(spread_kernel, out_shape=(jax.ShapeDtypeStruct((PER, N_GRO...]
    pallas_call x1 -> x0, Pallas kernels: 2.08 us -> none  [project(): pl.pallas_call(project_kernel, out_shape=(jax.ShapeDtypeStruct((N_CTX, PE...]
where the time goes in v3:
time: 116 us; the launch traced here: 115 us
  Pallas kernels  80.1 us (69%)
  blocking collectives  30.3 us (26%)
  local copies, waits for them, and re-layouts  4.4 us (4%)
    pallas_call x1, Pallas kernels, spread(): pl.pallas_call(spread_kernel, out_shape=(jax.ShapeDtypeStruct((PER, N_GRO...  48.6 us
    all_to_all x1, blocking collectives, on_device(): back = lax.all_to_all(att, 'ctx', split_axis=0, concat_axis=0, tiled=True)  30.3 us
    pallas_call x1, Pallas kernels, attend(): pl.pallas_call(attend_kernel, out_shape=jax.ShapeDtypeStruct((N_CTX, QROW...  29.7 us
    unnamed x16, local copies, waits for them, and re-layouts  3.03 us

profile of v3, /device:TPU:1, one launch (start us, length us, event | category | flops | bytes accessed | tf_op | source)
XLA Modules:
  0.0 114.9 jit_solution(10144310783283390515)
XLA Ops:
  0.0 0.7 reshape.14.token_ref
  0.7 0.7 reshape.15.gain_ref
  1.4 0.0 copy-start
  1.4 1.0 copy-done
  2.4 0.0 copy-start.3
  2.4 0.7 copy-done.3
  3.0 0.0 copy-start.5
  3.0 0.7 copy-done.5
  3.7 0.0 copy-start.7
  3.7 0.7 copy-done.7
  4.4 48.6 %spread.1 = (bf16[3,8,1024,128]{3,2,1,0:T(8,128)(2,1)S(1)}, bf16[32,48,128]{2,1,0:T(8,128)(2,1)S(1)}, s32[8,128]{1,0:T(8,128)S(1)}) custom-call(s32[8]{0:T(128)S(1)} %copy-done.5, bf16[8,32,768]{2,1,0:T(8,128)(2,1)S(1)} %bitcast.2, s32[1,256]{1,0:T(1,128)S(1)} %bitcast.3, bf16[1,768]{1,0:T(2,128)(2,1)S(1)} %reshape.14.token_ref, s32[1,256]{1,0:T(1,128)S(1)} %copy-done.7, ...), custom_call_target="tpu_custom_call" | custom-call | tf_op jit(solution)/shard_map/spread/pallas_call | solution.py:328
  53.0 0.0 copy-start.1
  53.0 0.0 copy-start.2
  53.0 0.0 copy-start.4
  53.0 0.0 copy-start.6
  53.1 29.7 %attend.1 = bf16[32,48,128]{2,1,0:T(8,128)(2,1)S(1)} custom-call(s32[8,128]{1,0:T(8,128)S(1)} %get-tuple-element.8.total_ref, bf16[32,48,128]{2,1,0:T(8,128)(2,1)S(1)} %get-tuple-element.9.q_ref, bf16[3,8,1024,128]{3,2,1,0:T(8,128)(2,1)S(1)} %get-tuple-element.10.kv), custom_call_target="tpu_custom_call" | custom-call | tf_op jit(solution)/shard_map/attend/pallas_call | solution.py:477
  82.8 30.3 %all_to_all.5.att_ref = bf16[32,48,128]{2,1,0:T(8,128)(2,1)S(1)} all-to-all(bf16[32,48,128]{2,1,0:T(8,128)(2,1)S(1)} %attend.1), channel_id=1, replica_groups=mesh['group'=8,'ctx'=32] {'ctx'}, dimensions={0} | all-to-all | bytes 786432 | tf_op jit(solution)/shard_map/all_to_all | solution.py:537
  113.1 0.0 copy-done.1
  113.1 0.0 copy-done.2
  113.1 0.0 copy-done.4
  113.1 0.0 copy-done.6
  113.1 1.8 %finish.1 = bf16[256,768]{1,0:T(8,128)(2,1)} custom-call(s32[8]{0:T(128)S(1)} %copy-done.6, bf16[32,48,128]{2,1,0:T(8,128)(2,1)S(1)} %all_to_all.5.att_ref, bf16[256,768]{1,0:T(8,128)(2,1)S(1)} %copy-done.1, s32[1,256]{1,0:T(1,128)S(1)} %bitcast.4, bf16[1,768]{1,0:T(2,128)(2,1)S(1)} %reshape.14.token_ref, bf16[768,768]{1,0:T(8,128)(2,1)S(1)} %copy-done.2), custom_call_target="tpu_custom_call" | custom-call | tf_op jit(solution)/shard_map/finish/pallas_call | solution.py:516
Async XLA Ops:
  1.4 1.0 copy-start
  2.4 0.7 copy-start.3
  3.0 0.7 copy-start.5
  3.7 0.7 copy-start.7
  53.0 60.1 %copy-start.1 = (bf16[256,768]{1,0:T(8,128)(2,1)S(1)}, bf16[256,768]{1,0:T(8,128)(2,1)}, u32[]{:S(2)}) copy-start(bf16[256,768]{1,0:T(8,128)(2,1)} %series_ref.1) | copy-start | bytes 1179652
  53.0 60.1 %copy-start.2 = (bf16[768,768]{1,0:T(8,128)(2,1)S(1)}, bf16[768,768]{1,0:T(8,128)(2,1)}, u32[]{:S(2)}) copy-start(bf16[768,768]{1,0:T(8,128)(2,1)} %w_ref.1) | copy-start | bytes 3538948
  53.0 60.0 %copy-start.4 = (s32[256]{0:T(256)S(1)}, s32[256]{0:T(256)}, u32[]{:S(2)}) copy-start(s32[256]{0:T(256)} %param.11) | copy-start | bytes 3076
  53.0 60.0 %copy-start.6 = (s32[8]{0:T(128)S(1)}, s32[8]{0:T(128)}, u32[]{:S(2)}) copy-start(s32[8]{0:T(128)} %packing_ref.3) | copy-start | bytes 100

commit v4 on v3

--- a/solution.py
+++ b/solution.py
@@ -48,7 +48,8 @@
 
 def masked_rows(rows, flags, token_ref):
     flags = jnp.concatenate([flags] * (D // 128), axis=1)
-    return jnp.where(flags == 1.0, token_ref[...].astype(jnp.float32), rows.astype(jnp.float32))
+    token = token_ref[...].astype(jnp.float32).reshape(1, D)
+    return jnp.where(flags == 1.0, token, rows.astype(jnp.float32))
 
 
 def normed_rows(packing_ref, series_ref, recon_ref, token_ref, gain_ref, flags):
@@ -61,7 +62,7 @@
         pieces.append(masked_rows(series_ref[at], flags[at], token_ref))
     x = jnp.concatenate(pieces, axis=0)
     factor = lax.rsqrt(jnp.mean(x * x, axis=-1, keepdims=True) + 1e-06)
-    return (x * factor * gain_ref[...].astype(jnp.float32)).astype(jnp.bfloat16)
+    return (x * factor * gain_ref[...].astype(jnp.float32).reshape(1, D)).astype(jnp.bfloat16)
 
 
 def document_counts(doc_ref):
@@ -108,9 +109,9 @@
 
 
 def spread_kernel(
-    packing_ref, series_ref, recon_ref, token_ref, doc_ref, gain_ref, wq_ref, wk_ref, wv_ref,
-    all_ref, qout_ref, total_ref,
-    kv_ref, q_ref, count_ref, flags, wq, wk, wv, w_sem, counts, kv_send, kv_recv, q_send, q_recv, c_send, c_recv, self_sem,
+    packing_hbm, token_hbm, gain_hbm, series_hbm, recon_hbm, doc_hbm, wq_ref, wk_ref, wv_ref,
+    k1_ref, vt_ref, qout_ref, total_ref, norm_ref,
+    packing_ref, token_ref, gain_ref, series_ref, recon_ref, doc_ref, all_ref, norms, kv_ref, q_ref, count_ref, flags, wq, wk, wv, w_sem, counts, kv_send, kv_recv, q_send, q_recv, c_send, c_recv, self_sem,
     x_send, near_recv, half_recv, pair_recv, t_send, t_recv,
 ):
     s = lax.axis_index("group")
@@ -119,6 +120,16 @@
     partner = s + 1 - 2 * lax.rem(s, 2)
     right, left, across = lax.rem(s + 2, N_GROUP), lax.rem(s + 6, N_GROUP), lax.rem(s + 4, N_GROUP)
     owner = z == s
+    loads = [
+        pltpu.make_async_copy(src, dst, w_sem.at[n])
+        for n, (src, dst) in enumerate((
+            (wk_ref, wk), (wv_ref, wv), (wq_ref, wq),
+            (series_hbm, series_ref), (recon_hbm, recon_ref), (doc_hbm, doc_ref),
+            (packing_hbm, packing_ref), (token_hbm, token_ref), (gain_hbm, gain_ref),
+        ))
+    ]
+    for n in (3, 4, 5, 6, 7, 8, 0, 1, 2):
+        loads[n].start()
     bar = pltpu.get_barrier_semaphore()
 
     def greet(o, carry):
@@ -128,12 +139,10 @@
     lax.fori_loop(1, N_CTX, greet, 0)
     for o in range(1, N_GROUP):
         pl.semaphore_signal(bar, inc=1, device_id=(lax.rem(s + o, N_GROUP), c), device_id_type=MESH)
-    loads = [
-        pltpu.make_async_copy(src, dst, w_sem.at[n])
-        for n, (src, dst) in enumerate(((wk_ref, wk), (wv_ref, wv), (wq_ref, wq)))
-    ]
-    for load in loads:
-        load.start()
+    vt_ref[:, :, 0:16, :] = jnp.ones((PER, N_Z, 16, ROWS), jnp.bfloat16)
+    norms[...] = jnp.zeros_like(norms)
+    for n in range(3, 9):
+        loads[n].wait()
     count_ref[...] = document_counts(doc_ref)
     normed = normed_rows(packing_ref, series_ref, recon_ref, token_ref, gain_ref, flags)
 
@@ -178,6 +187,11 @@
     own_kv = pltpu.make_async_copy(kv_ref.at[c], all_ref.at[:, s, rows_of(c), :], self_sem.at[0])
     own_q = pltpu.make_async_copy(q_ref.at[c], qout_ref.at[c], self_sem.at[1])
     own_kv.start()
+    for t in range(N_Y):
+        @pl.when(s * N_Y + t != c)
+        def _():
+            send_count(t).start()
+
     for yy in range(1, N_Y):
         send_kv(other(0, yy), 0).start()
 
@@ -186,13 +200,7 @@
             send_kv(other(i, yy), i).start()
         return carry
 
-    lax.fori_loop(1, 3, start_plane, 0)
-    for t in range(N_Y):
-        @pl.when(s * N_Y + t != c)
-        def _():
-            send_count(t).start()
-
-    lax.fori_loop(3, N_Z, start_plane, 0)
+    lax.fori_loop(1, N_Z, start_plane, 0)
     pack_queries(q_ref, project(2, wq) * SCALE)
     own_q.start()
 
@@ -201,9 +209,6 @@
             send_q(other(i, yy)).start()
         return carry
 
-    for yy in range(1, N_Y):
-        send_q(other(0, yy)).start()
-    lax.fori_loop(1, N_Z, start_q, 0)
 
     def plane(i):
         return lax.rem(z + N_Z - step_z(i), N_Z)
@@ -228,20 +233,47 @@
     def send_own(i):
         hop(s, i, right, 0, near_recv.at[0, i]).start()
         hop(s, i, left, 1, near_recv.at[1, i]).start()
-        hop(s, i, partner, 2, pair_recv.at[0]).start()
+        hop(s, i, partner, 2, pair_recv.at[0, i]).start()
 
     def send_near(i):
         hop(left, i, left, 0, near_recv.at[0, i]).wait_recv()
         hop(left, i, right, 3, half_recv.at[0, i], half=0).start()
-        hop(left, i, partner, 5, pair_recv.at[1]).start()
+        hop(left, i, partner, 5, pair_recv.at[1, i]).start()
         hop(right, i, right, 1, near_recv.at[1, i]).wait_recv()
         hop(right, i, left, 4, half_recv.at[1, i], half=1).start()
-        hop(right, i, partner, 6, pair_recv.at[2]).start()
+        hop(right, i, partner, 6, pair_recv.at[2, i]).start()
 
     def send_across(i):
         hop(across, i, left, 3, half_recv.at[0, i], half=0).wait_recv()
         hop(across, i, right, 4, half_recv.at[1, i], half=1).wait_recv()
-        hop(across, i, partner, 7, pair_recv.at[3]).start()
+        hop(across, i, partner, 7, pair_recv.at[3, i]).start()
+
+    slots = (partner, lax.rem(partner + 6, N_GROUP), lax.rem(partner + 2, N_GROUP), lax.rem(partner + 4, N_GROUP))
+    r = lax.broadcasted_iota(jnp.int32, (128, 128), 0)
+    base = ((r // BLK) * 256 + r % BLK).astype(jnp.float32)
+    lane = lax.broadcasted_iota(jnp.int32, (1, 128), 1)
+    low = low_half((128, 128))
+
+    def lay_out(i):
+        for n, slot in enumerate(slots):
+            hop(slot, i, partner, 2, pair_recv.at[n, i]).wait_recv()
+        at = plane(i)
+        rows = pl.ds(pl.multiple_of(at * 128, 128), 128)
+        totals = total_ref[...].astype(jnp.float32)
+        lo = pltpu.roll(totals, HD + 1, 1)[0:1]
+        hi = jnp.where(lane == HD + DOCS - 1, float(N_CTX * 256), pltpu.roll(totals, HD, 1)[0:1])
+        first = (at * 1024).astype(jnp.float32)
+        lo, hi = lo - first, hi - first
+        for n in range(N_GROUP):
+            own = (base >= lo - n * BLK) & (base < hi - n * BLK)
+            mark = jnp.where(own, 1.0, 0.0).astype(jnp.bfloat16)
+            for h in range(PER):
+                k1_ref[h, n, rows, :] = jnp.where(low, all_ref[h, n, rows, :], mark)
+        for h in range(PER):
+            block = all_ref[h, :, rows, :].reshape(ROWS, 128).T
+            vt_ref[h, at, 16:80, :] = block[HD:128]
+            keys = block[0:HD].astype(jnp.float32)
+            norms[h] = jnp.maximum(norms[h], jnp.sum(keys * keys, axis=0, keepdims=True))
 
     def arrive_plane(i):
         part = all_ref.at[:, s, pl.ds(pl.multiple_of(plane(i) * 128, 128), 128), :]
@@ -260,15 +292,21 @@
     arrive_plane(1)
     send_own(1)
     send_near(0)
+    for yy in range(1, N_Y):
+        send_q(other(0, yy)).start()
+    lax.fori_loop(1, N_Z, start_q, 0)
+    arrive_plane(2)
+    send_own(2)
+    send_near(1)
+    send_across(0)
 
     def step(i, carry):
         arrive_plane(i)
         send_own(i)
         send_near(i - 1)
         send_across(i - 2)
+        lay_out(i - 3)
         return carry
-
-    lax.fori_loop(2, 5, step, 0)
 
     @pl.when(owner)
     def _():
@@ -282,10 +320,22 @@
         for o in range(1, N_GROUP):
             send_total(o).start()
 
-    lax.fori_loop(5, N_Z, step, 0)
+    @pl.when(jnp.logical_not(owner))
+    def _():
+        send_total(1).wait_recv()
+
+    lax.fori_loop(3, N_Z, step, 0)
     send_near(N_Z - 1)
     send_across(N_Z - 2)
+    lay_out(N_Z - 3)
     send_across(N_Z - 1)
+    lay_out(N_Z - 2)
+    lay_out(N_Z - 1)
+    sub = lax.broadcasted_iota(jnp.int32, (8, 128), 0)
+    top = jnp.zeros((8, 128), jnp.float32)
+    for h in range(PER):
+        top = jnp.where(sub == h, jnp.max(norms[h], axis=1, keepdims=True), top)
+    norm_ref[...] = top
 
     for t in range(N_Y):
         @pl.when(s * N_Y + t != c)
@@ -296,10 +346,6 @@
     def _():
         for o in range(1, N_GROUP):
             send_total(o).wait_send()
-
-    @pl.when(jnp.logical_not(owner))
-    def _():
-        send_total(1).wait_recv()
 
     own_q.wait()
     rest = pltpu.make_async_remote_copy(
@@ -315,9 +361,10 @@
     ).wait_send()
     for kind, slot in enumerate((s, s, s, left, right, left, right, across)):
         whole(slot, kind, t_recv, half=0 if kind in (3, 4) else None).wait_send()
-    slots = (partner, lax.rem(partner + 6, N_GROUP), lax.rem(partner + 2, N_GROUP), lax.rem(partner + 4, N_GROUP))
-    for n, slot in enumerate(slots):
-        whole(slot, 2, pair_recv.at[n]).wait_recv()
+
+
+def hbm(x):
+    return pltpu.with_memory_space_constraint(x, pltpu.HBM)
 
 
 def spread(packing, series, recon, token, docs, gain, w_query, w_key, w_value):
@@ -329,30 +376,40 @@
         spread_kernel,
         out_shape=(
             jax.ShapeDtypeStruct((PER, N_GROUP, ROWS, 128), jnp.bfloat16),
+            jax.ShapeDtypeStruct((PER, N_Z, 80, ROWS), jnp.bfloat16),
             jax.ShapeDtypeStruct((N_CTX, QROWS, 128), jnp.bfloat16),
             jax.ShapeDtypeStruct((8, 128), jnp.int32),
+            jax.ShapeDtypeStruct((8, 128), jnp.float32),
         ),
-        in_specs=[pl.BlockSpec(memory_space=pltpu.SMEM)] + [vmem] * 5 + [anywhere] * 3,
-        out_specs=(anywhere, anywhere, vmem),
+        in_specs=[anywhere] * 9,
+        out_specs=(vmem, vmem, anywhere, vmem, vmem),
         scratch_shapes=[
+            pltpu.SMEM((N_GROUP,), jnp.int32),
+            pltpu.VMEM((D,), jnp.bfloat16),
+            pltpu.VMEM((D,), jnp.bfloat16),
+            pltpu.VMEM((N_GROUP, BLK, D), jnp.bfloat16),
+            pltpu.VMEM((1, N_GROUP * BLK), jnp.int32),
+            pltpu.VMEM((1, N_GROUP * BLK), jnp.int32),
+            pltpu.VMEM((PER, N_GROUP, ROWS, 128), jnp.bfloat16),
+            pltpu.VMEM((PER, 1, ROWS), jnp.float32),
             pltpu.VMEM((N_CTX, PER, BLK, 128), jnp.bfloat16),
             pltpu.VMEM((N_CTX, QROWS, 128), jnp.bfloat16),
             pltpu.VMEM((8, 128), jnp.int32),
             pltpu.VMEM((N_GROUP, BLK, 128), jnp.float32),
             weight, weight, weight,
-            dma((3,)),
+            dma((9,)),
             pltpu.VMEM((N_CTX, 8, 128), jnp.int32),
             dma(()), dma((N_Z,)), dma(()), dma(()), dma((N_Y,)), dma(()), dma((2,)),
-            dma((8,)), dma((2, N_Z)), dma((2, N_Z)), dma((4,)), dma((N_GROUP - 1,)), dma(()),
+            dma((8,)), dma((2, N_Z)), dma((2, N_Z)), dma((4, N_Z)), dma((N_GROUP - 1,)), dma(()),
         ],
         compiler_params=pltpu.CompilerParams(
             collective_id=0, has_side_effects=True, vmem_limit_bytes=32 << 20
         ),
         name="spread",
-    )(packing, series, recon, token, docs, gain, w_query, w_key, w_value)
-
-
-def attend_kernel(total_ref, q_ref, kv, out_ref, qt, k1, vt, acc, top):
+    )(*(hbm(x) for x in (packing, token, gain, series, recon, docs, w_query, w_key, w_value)))
+
+
+def attend_kernel(total_ref, norm_ref, q_ref, k1, vt, out_ref, qt, acc, top):
     s = lax.axis_index("group")
     starts = [total_ref[0, d] for d in range(3)]
     first, last = [jnp.int32(0)] + starts, starts + [jnp.int32(N_CTX * 256)]
@@ -380,29 +437,10 @@
         q_top.append(jnp.max(jnp.sum(part * part, axis=0, keepdims=True)))
         qt[h] = jnp.concatenate([part, far], axis=0).astype(jnp.bfloat16)
 
-    r = lax.broadcasted_iota(jnp.int32, (ROWS, 128), 0)
-    base = (r // BLK) * 256 + r % BLK
-    lo, hi = edges(lax.broadcasted_iota(jnp.int32, (1, 128), 1))
     keys_n = KC * 256
-    low = low_half((ROWS, 128))
-    vt[:, :, 0:16, :] = jnp.ones((PER, N_CTX // KC, 16, keys_n), jnp.bfloat16)
     small = None
     for h in range(PER):
-        for n in range(N_GROUP):
-            both = kv[h, n]
-            if h == 0:
-                own = (base >= lo - n * BLK) & (base < hi - n * BLK)
-                mark = jnp.where(own, 1.0, 0.0).astype(jnp.bfloat16)
-            else:
-                mark = k1[0, n]
-            k1[h, n] = jnp.where(low, both, mark)
-        norms = jnp.zeros((1, keys_n), jnp.float32)
-        for kb in range(N_CTX // KC):
-            block = kv[h, :, kb * KC * BLK : (kb + 1) * KC * BLK, :].reshape(keys_n, 128).T
-            vt[h, kb, 16:80, :] = block[HD:128]
-            keys = block[0:HD].astype(jnp.float32)
-            norms = jnp.maximum(norms, jnp.sum(keys * keys, axis=0, keepdims=True))
-        fits = q_top[h] * jnp.max(norms) * 1.05 <= BOUND * BOUND
+        fits = q_top[h] * norm_ref[h, 0] * 1.05 <= BOUND * BOUND
         small = fits if small is None else small & fits
 
     span = TQ // BLK * 256
@@ -471,24 +509,22 @@
     lax.fori_loop(0, ROWS // TQ, tile, 0)
 
 
-def attend(total, q, kv):
+def attend(total, norms, q, k1, vt):
     vmem = pl.BlockSpec(memory_space=pltpu.VMEM)
-    wide = pltpu.VMEM((PER, N_GROUP, ROWS, 128), jnp.bfloat16)
+    smem = pl.BlockSpec(memory_space=pltpu.SMEM)
     return pl.pallas_call(
         attend_kernel,
         out_shape=jax.ShapeDtypeStruct((N_CTX, QROWS, 128), jnp.bfloat16),
-        in_specs=[pl.BlockSpec(memory_space=pltpu.SMEM), vmem, vmem],
+        in_specs=[smem, smem, vmem, vmem, vmem],
         out_specs=vmem,
         scratch_shapes=[
             pltpu.VMEM((PER, 128, ROWS), jnp.bfloat16),
-            wide,
-            pltpu.VMEM((PER, N_CTX // KC, 80, KC * 256), jnp.bfloat16),
             pltpu.VMEM((PER, 80, TQ), jnp.float32),
             pltpu.VMEM((PER, 1, TQ), jnp.float32),
         ],
-        compiler_params=pltpu.CompilerParams(vmem_limit_bytes=40 << 20),
+        compiler_params=pltpu.CompilerParams(vmem_limit_bytes=32 << 20),
         name="attend",
-    )(total, q, kv)
+    )(total, norms, q, k1, vt)
 
 
 def finish_kernel(packing_ref, att_ref, series_ref, recon_ref, token_ref, w_ref, out_ref, lhs, w2):
@@ -528,12 +564,12 @@
     series, recon_mask, mask_token, packing_list, doc_ids, norm_gain, w_query, w_key, w_value, w_out
 ):
     recon = recon_mask.reshape(1, -1)
-    token = mask_token.reshape(1, -1)
-    all_kv, q_rows, total = spread(
-        packing_list, series.reshape(N_GROUP, BLK, D), recon, token, doc_ids, norm_gain.reshape(1, -1),
-        *(pltpu.with_memory_space_constraint(w, pltpu.HBM) for w in (w_query, w_key, w_value)),
+    token = mask_token
+    k1, vt, q_rows, total, norms = spread(
+        packing_list, series.reshape(N_GROUP, BLK, D), recon, token, doc_ids, norm_gain,
+        w_query, w_key, w_value,
     )
-    att = attend(total, q_rows, all_kv)
+    att = attend(total, norms, q_rows, k1, vt)
     back = lax.all_to_all(att, "ctx", split_axis=0, concat_axis=0, tiled=True)
     return finish(packing_list, back, series, recon, token, w_out)
 

time: 116 us -> 104 us (0.90)
  blocking collectives: 30.3 us -> 20.4 us
  local copies, waits for them, and re-layouts: 4.4 us -> 0.03 us
  Pallas kernels: 80.1 us -> 83.4 us
    all_to_all x1, blocking collectives: 30.3 us -> 20.4 us  [on_device(): back = lax.all_to_all(att, 'ctx', split_axis=0, concat_axis=0, tiled=True)]
    unnamed x16 -> x10, local copies, waits for them, and re-layouts: 3.03 us -> 0.03 us
    pallas_call x1, Pallas kernels: 48.6 us -> 51.5 us  [spread(): pl.pallas_call(spread_kernel, out_shape=(jax.ShapeDtypeStruct((PER, N_GRO...]
    reshape x2 -> x0, local copies, waits for them, and re-layouts: 1.37 us -> none  [the longest x1 0.68 us: on_device(): token = mask_token.reshape(1, -1)]
where the time goes in v4:
time: 104 us
  Pallas kernels  83.4 us (80%)
  blocking collectives  20.4 us (20%)
    pallas_call x1, Pallas kernels, spread(): pl.pallas_call(spread_kernel, out_shape=(jax.ShapeDtypeStruct((PER, N_GRO...  51.5 us
    pallas_call x1, Pallas kernels, attend(): pl.pallas_call(attend_kernel, out_shape=jax.ShapeDtypeStruct((N_CTX, QROW...  30.1 us
    all_to_all x1, blocking collectives, on_device(): back = lax.all_to_all(att, 'ctx', split_axis=0, concat_axis=0, tiled=True)  20.4 us

profile of v4, /device:TPU:1, one launch (start us, length us, event | category | flops | bytes accessed | tf_op | source)
XLA Modules:
  0.0 104.0 jit_solution(5462171068810818471)
XLA Ops:
  0.0 51.5 %spread.1 = (bf16[3,8,1024,128]{3,2,1,0:T(8,128)(2,1)S(1)}, bf16[3,8,80,1024]{3,2,1,0:T(8,128)(2,1)S(1)}, bf16[32,48,128]{2,1,0:T(8,128)(2,1)S(1)}, s32[8,128]{1,0:T(8,128)S(1)}, f32[8,128]{1,0:T(8,128)S(1)}) custom-call(s32[8]{0:T(128)} %packing_ref.1, bf16[768]{0:T(1024)(128)(2,1)} %token_ref.1, bf16[768]{0:T(1024)(128)(2,1)} %gain_hbm.1, ...), custom_call_target="tpu_custom_call" | custom-call | tf_op jit(solution)/shard_map/spread/pallas_call | solution.py:375
  51.5 0.0 copy-start
  51.5 0.0 copy-start.1
  51.5 0.0 copy-start.2
  51.5 0.0 copy-start.3
  51.5 0.0 copy-start.4
  51.5 30.1 %attend.1 = bf16[32,48,128]{2,1,0:T(8,128)(2,1)S(1)} custom-call(s32[8,128]{1,0:T(8,128)S(1)} %get-tuple-element.10.total_ref, f32[8,128]{1,0:T(8,128)S(1)} %get-tuple-element.11.norm_ref, bf16[32,48,128]{2,1,0:T(8,128)(2,1)S(1)} %get-tuple-element.12.q_ref, bf16[3,8,1024,128]{3,2,1,0:T(8,128)(2,1)S(1)} %get-tuple-element.13.k1, ...), custom_call_target="tpu_custom_call" | custom-call | tf_op jit(solution)/shard_map/attend/pallas_call | solution.py:515
  81.7 20.4 %all_to_all.5.att_ref = bf16[32,48,128]{2,1,0:T(8,128)(2,1)S(1)} all-to-all(bf16[32,48,128]{2,1,0:T(8,128)(2,1)S(1)} %attend.1), channel_id=1, replica_groups=mesh['group'=8,'ctx'=32] {'ctx'}, dimensions={0} | all-to-all | bytes 786432 | tf_op jit(solution)/shard_map/all_to_all | solution.py:573
  102.1 0.0 copy-done
  102.1 0.0 copy-done.1
  102.1 0.0 copy-done.2
  102.1 0.0 copy-done.3
  102.1 0.0 copy-done.4
  102.2 1.8 %finish.1 = bf16[256,768]{1,0:T(8,128)(2,1)} custom-call(s32[8]{0:T(128)S(1)} %copy-done.4, bf16[32,48,128]{2,1,0:T(8,128)(2,1)S(1)} %all_to_all.5.att_ref, bf16[256,768]{1,0:T(8,128)(2,1)S(1)} %copy-done, s32[1,256]{1,0:T(1,128)S(1)} %bitcast.4, bf16[768]{0:T(1024)(128)(2,1)S(1)} %copy-done.2, bf16[768,768]{1,0:T(8,128)(2,1)S(1)} %copy-done.1), custom_call_target="tpu_custom_call" | custom-call | tf_op jit(solution)/shard_map/finish/pallas_call | solution.py:552
Async XLA Ops:
  51.5 50.6 %copy-start = (bf16[256,768]{1,0:T(8,128)(2,1)S(1)}, bf16[256,768]{1,0:T(8,128)(2,1)}, u32[]{:S(2)}) copy-start(bf16[256,768]{1,0:T(8,128)(2,1)} %series_ref.1) | copy-start | bytes 1179652
  51.5 50.6 %copy-start.1 = (bf16[768,768]{1,0:T(8,128)(2,1)S(1)}, bf16[768,768]{1,0:T(8,128)(2,1)}, u32[]{:S(2)}) copy-start(bf16[768,768]{1,0:T(8,128)(2,1)} %w_ref.1) | copy-start | bytes 3538948
  51.5 50.6 %copy-start.2 = (bf16[768]{0:T(1024)(128)(2,1)S(1)}, bf16[768]{0:T(1024)(128)(2,1)}, u32[]{:S(2)}) copy-start(bf16[768]{0:T(1024)(128)(2,1)} %token_ref.1) | copy-start | bytes 4612
  51.5 50.6 %copy-start.3 = (s32[256]{0:T(256)S(1)}, s32[256]{0:T(256)}, u32[]{:S(2)}) copy-start(s32[256]{0:T(256)} %param.11) | copy-start | bytes 3076
  51.5 50.6 %copy-start.4 = (s32[8]{0:T(128)S(1)}, s32[8]{0:T(128)}, u32[]{:S(2)}) copy-start(s32[8]{0:T(128)} %packing_ref.1) | copy-start | bytes 100

commit v5 on v4

--- a/solution.py
+++ b/solution.py
@@ -527,24 +527,64 @@
     )(total, norms, q, k1, vt)
 
 
-def finish_kernel(packing_ref, att_ref, series_ref, recon_ref, token_ref, w_ref, out_ref, lhs, w2):
+def finish_kernel(
+    packing_ref, att_ref, series_ref, recon_ref, token_ref, w_ref, out_ref,
+    got, lhs, w2, self_sem, send_sem, recv_sem,
+):
+    s = lax.axis_index("group")
+    c = lax.axis_index("ctx")
+    z, y = c // N_Y, lax.rem(c, N_Y)
+    bar = pltpu.get_barrier_semaphore()
+
+    def greet(o, carry):
+        pl.semaphore_signal(bar, inc=1, device_id=(s, lax.rem(c + o, N_CTX)), device_id_type=MESH)
+        return carry
+
+    lax.fori_loop(1, N_CTX, greet, 0)
+    own = pltpu.make_async_copy(att_ref.at[c], got.at[c], self_sem)
+    own.start()
+
+    def send(i, yy):
+        d = lax.rem(z + step_z(i), N_Z) * N_Y + lax.rem(y + yy, N_Y)
+        pltpu.make_async_remote_copy(
+            src_ref=att_ref.at[d], dst_ref=got.at[c], send_sem=send_sem, recv_sem=recv_sem,
+            device_id=(s, d), device_id_type=MESH,
+        ).start()
+
+    def send_plane(i, carry):
+        for yy in range(N_Y):
+            send(i, yy)
+        return carry
+
+    pl.semaphore_wait(bar, N_CTX - 1)
+    lax.fori_loop(1, N_Z, send_plane, 0)
+    for yy in range(1, N_Y):
+        send(0, yy)
     order = [PER * t + n for t in range(TRIPLES) for n in range(2)] + [2, 5, 8, 11]
     for n, head in enumerate(order):
         w2[n * HD : (n + 1) * HD, :] = w_ref[head * HD : (head + 1) * HD, :]
+    residual = masked_rows(series_ref[...], row_mask(recon_ref), token_ref)
+    own.wait()
+    rest = pltpu.make_async_remote_copy(
+        src_ref=att_ref.at[pl.ds(0, N_CTX - 1)], dst_ref=got.at[pl.ds(0, N_CTX - 1)],
+        send_sem=send_sem, recv_sem=recv_sem, device_id=(s, lax.rem(c + 1, N_CTX)), device_id_type=MESH,
+    )
+    rest.wait_recv()
+    rest.wait_send()
     for k in range(N_GROUP):
         g = packing_ref[k]
+        parts = [got[g * TRIPLES + t] for t in range(TRIPLES)]
         rows = slice(k * BLK, (k + 1) * BLK)
         for t in range(TRIPLES):
-            lhs[rows, t * 128 : (t + 1) * 128] = att_ref[g * TRIPLES + t, 0:BLK]
+            lhs[rows, t * 128 : (t + 1) * 128] = parts[t][0:BLK]
         for n in range(2):
-            a = att_ref[g * TRIPLES + 2 * n, BLK:QROWS].astype(jnp.float32)
-            b = att_ref[g * TRIPLES + 2 * n + 1, BLK:QROWS].astype(jnp.float32)
+            a = parts[2 * n][BLK:QROWS].astype(jnp.float32)
+            b = parts[2 * n + 1][BLK:QROWS].astype(jnp.float32)
             cols = slice((TRIPLES + n) * 128, (TRIPLES + n + 1) * 128)
             lhs[k * BLK : k * BLK + 16, cols] = join(a, swap(b)).astype(jnp.bfloat16)
             lhs[k * BLK + 16 : (k + 1) * BLK, cols] = join(swap(a), b).astype(jnp.bfloat16)
     mixed = jnp.dot(lhs[...], w2[...], preferred_element_type=jnp.float32)
-    rows = masked_rows(series_ref[...], row_mask(recon_ref), token_ref)
-    out_ref[...] = (rows + mixed).astype(jnp.bfloat16)
+    out_ref[...] = (residual + mixed).astype(jnp.bfloat16)
 
 
 def finish(packing, att, series, recon, token, w_out):
@@ -554,8 +594,17 @@
         out_shape=jax.ShapeDtypeStruct(series.shape, jnp.bfloat16),
         in_specs=[pl.BlockSpec(memory_space=pltpu.SMEM)] + [vmem] * 5,
         out_specs=vmem,
-        scratch_shapes=[pltpu.VMEM((N_GROUP * BLK, D), jnp.bfloat16), pltpu.VMEM((D, D), jnp.bfloat16)],
-        compiler_params=pltpu.CompilerParams(vmem_limit_bytes=48 << 20),
+        scratch_shapes=[
+            pltpu.VMEM((N_CTX, QROWS, 128), jnp.bfloat16),
+            pltpu.VMEM((N_GROUP * BLK, D), jnp.bfloat16),
+            pltpu.VMEM((D, D), jnp.bfloat16),
+            pltpu.SemaphoreType.DMA,
+            pltpu.SemaphoreType.DMA,
+            pltpu.SemaphoreType.DMA,
+        ],
+        compiler_params=pltpu.CompilerParams(
+            collective_id=1, has_side_effects=True, vmem_limit_bytes=48 << 20
+        ),
         name="finish",
     )(packing, att, series, recon, token, w_out)
 
@@ -570,8 +619,7 @@
         w_query, w_key, w_value,
     )
     att = attend(total, norms, q_rows, k1, vt)
-    back = lax.all_to_all(att, "ctx", split_axis=0, concat_axis=0, tiled=True)
-    return finish(packing_list, back, series, recon, token, w_out)
+    return finish(packing_list, att, series, recon, token, w_out)
 
 
 def solution(mesh):

time: 104 us -> 102 us (0.981)
  blocking collectives: 20.4 us -> 0 us
  Pallas kernels: 83.4 us -> 101 us
    all_to_all x1 -> x0, blocking collectives: 20.4 us -> none  [on_device(): back = lax.all_to_all(att, 'ctx', split_axis=0, concat_axis=0, tiled=True)]
    pallas_call x1, Pallas kernels: 1.8 us -> 19.3 us  [finish(): pl.pallas_call(finish_kernel, out_shape=jax.ShapeDtypeStruct(series.shape...]
where the time goes in v5:
time: 102 us
  Pallas kernels  101 us (99%)
    pallas_call x1, Pallas kernels, spread(): pl.pallas_call(spread_kernel, out_shape=(jax.ShapeDtypeStruct((PER, N_GRO...  51.5 us
    pallas_call x1, Pallas kernels, attend(): pl.pallas_call(attend_kernel, out_shape=jax.ShapeDtypeStruct((N_CTX, QROW...  30.1 us
    pallas_call x1, Pallas kernels, finish(): pl.pallas_call(finish_kernel, out_shape=jax.ShapeDtypeStruct(series.shape...  19.3 us

profile of v5, /device:TPU:1, one launch (start us, length us, event | category | flops | bytes accessed | tf_op | source)
XLA Modules:
  0.0 101.8 jit_solution(1325372101463950337)
XLA Ops:
  0.0 51.5 %spread.1 = (bf16[3,8,1024,128]{3,2,1,0:T(8,128)(2,1)S(1)}, bf16[3,8,80,1024]{3,2,1,0:T(8,128)(2,1)S(1)}, bf16[32,48,128]{2,1,0:T(8,128)(2,1)S(1)}, s32[8,128]{1,0:T(8,128)S(1)}, f32[8,128]{1,0:T(8,128)S(1)}) custom-call(s32[8]{0:T(128)} %packing_ref.1, bf16[768]{0:T(1024)(128)(2,1)} %token_ref.1, bf16[768]{0:T(1024)(128)(2,1)} %gain_hbm.1, ...), custom_call_target="tpu_custom_call" | custom-call | tf_op jit(solution)/shard_map/spread/pallas_call | solution.py:375
  51.5 0.0 copy-start
  51.5 0.0 copy-start.1
  51.5 0.0 copy-start.2
  51.5 0.0 copy-start.3
  51.5 0.0 copy-start.4
  51.5 30.1 %attend.1.att_ref = bf16[32,48,128]{2,1,0:T(8,128)(2,1)S(1)} custom-call(s32[8,128]{1,0:T(8,128)S(1)} %get-tuple-element.10.total_ref, f32[8,128]{1,0:T(8,128)S(1)} %get-tuple-element.11.norm_ref, bf16[32,48,128]{2,1,0:T(8,128)(2,1)S(1)} %get-tuple-element.12.q_ref, bf16[3,8,1024,128]{3,2,1,0:T(8,128)(2,1)S(1)} %get-tuple-element.13.k1, ...), custom_call_target="tpu_custom_call" | custom-call | tf_op jit(solution)/shard_map/attend/pallas_call | solution.py:515
  81.7 0.0 copy-done
  81.7 0.0 copy-done.1
  81.7 0.0 copy-done.2
  81.7 0.0 copy-done.3
  81.7 0.0 copy-done.4
  81.7 19.3 %finish.1 = bf16[256,768]{1,0:T(8,128)(2,1)S(1)} custom-call(s32[8]{0:T(128)S(1)} %copy-done.4, bf16[32,48,128]{2,1,0:T(8,128)(2,1)S(1)} %attend.1.att_ref, bf16[256,768]{1,0:T(8,128)(2,1)S(1)} %copy-done, s32[1,256]{1,0:T(1,128)S(1)} %bitcast.4, bf16[768]{0:T(1024)(128)(2,1)S(1)} %copy-done.2, bf16[768,768]{1,0:T(8,128)(2,1)S(1)} %copy-done.1), custom_call_target="tpu_custom_call" | custom-call | tf_op jit(solution)/shard_map/finish/pallas_call | solution.py:592
  101.0 0.7 copy.12
Async XLA Ops:
  51.5 30.2 %copy-start = (bf16[256,768]{1,0:T(8,128)(2,1)S(1)}, bf16[256,768]{1,0:T(8,128)(2,1)}, u32[]{:S(2)}) copy-start(bf16[256,768]{1,0:T(8,128)(2,1)} %series_ref.1) | copy-start | bytes 1179652
  51.5 30.2 %copy-start.1 = (bf16[768,768]{1,0:T(8,128)(2,1)S(1)}, bf16[768,768]{1,0:T(8,128)(2,1)}, u32[]{:S(2)}) copy-start(bf16[768,768]{1,0:T(8,128)(2,1)} %w_ref.1) | copy-start | bytes 3538948
  51.5 30.2 %copy-start.2 = (bf16[768]{0:T(1024)(128)(2,1)S(1)}, bf16[768]{0:T(1024)(128)(2,1)}, u32[]{:S(2)}) copy-start(bf16[768]{0:T(1024)(128)(2,1)} %token_ref.1) | copy-start | bytes 4612
  51.5 30.2 %copy-start.3 = (s32[256]{0:T(256)S(1)}, s32[256]{0:T(256)}, u32[]{:S(2)}) copy-start(s32[256]{0:T(256)} %param.11) | copy-start | bytes 3076
  51.5 30.2 %copy-start.4 = (s32[8]{0:T(128)S(1)}, s32[8]{0:T(128)}, u32[]{:S(2)}) copy-start(s32[8]{0:T(128)} %packing_ref.1) | copy-start | bytes 100

commit v6 on v5

--- a/solution.py
+++ b/solution.py
@@ -200,7 +200,7 @@
             send_kv(other(i, yy), i).start()
         return carry
 
-    lax.fori_loop(1, N_Z, start_plane, 0)
+    lax.fori_loop(1, 5, start_plane, 0)
     pack_queries(q_ref, project(2, wq) * SCALE)
     own_q.start()
 
@@ -289,6 +289,7 @@
         device_id=(partner, c), device_id_type=MESH,
     ).wait_recv()
     send_own(0)
+    lax.fori_loop(5, N_Z, start_plane, 0)
     arrive_plane(1)
     send_own(1)
     send_near(0)
@@ -320,11 +321,17 @@
         for o in range(1, N_GROUP):
             send_total(o).start()
 
+    arrive_plane(3)
+    send_own(3)
+    send_near(2)
+    send_across(1)
+
     @pl.when(jnp.logical_not(owner))
     def _():
         send_total(1).wait_recv()
 
-    lax.fori_loop(3, N_Z, step, 0)
+    lay_out(0)
+    lax.fori_loop(4, N_Z, step, 0)
     send_near(N_Z - 1)
     send_across(N_Z - 2)
     lay_out(N_Z - 3)

time: 102 us -> 103 us (level); the launches traced: 102 us -> 101 us
    pallas_call x1, Pallas kernels: 19.3 us -> 26.7 us  [finish(): pl.pallas_call(finish_kernel, out_shape=jax.ShapeDtypeStruct(series.shape...]
    pallas_call x1, Pallas kernels: 30.1 us -> 24.9 us  [attend(): pl.pallas_call(attend_kernel, out_shape=jax.ShapeDtypeStruct((N_CTX, QROW...]
    pallas_call x1, Pallas kernels: 51.5 us -> 48.9 us  [spread(): pl.pallas_call(spread_kernel, out_shape=(jax.ShapeDtypeStruct((PER, N_GRO...]
where the time goes in v6:
time: 103 us; the launch traced here: 101 us
  Pallas kernels  101 us (98%)
    pallas_call x1, Pallas kernels, spread(): pl.pallas_call(spread_kernel, out_shape=(jax.ShapeDtypeStruct((PER, N_GRO...  48.9 us
    pallas_call x1, Pallas kernels, finish(): pl.pallas_call(finish_kernel, out_shape=jax.ShapeDtypeStruct(series.shape...  26.7 us
    pallas_call x1, Pallas kernels, attend(): pl.pallas_call(attend_kernel, out_shape=jax.ShapeDtypeStruct((N_CTX, QROW...  24.9 us

profile of v6, /device:TPU:1, one launch (start us, length us, event | category | flops | bytes accessed | tf_op | source)
XLA Modules:
  0.0 101.4 jit_solution(2604541624345279489)
XLA Ops:
  0.0 48.9 %spread.1 = (bf16[3,8,1024,128]{3,2,1,0:T(8,128)(2,1)S(1)}, bf16[3,8,80,1024]{3,2,1,0:T(8,128)(2,1)S(1)}, bf16[32,48,128]{2,1,0:T(8,128)(2,1)S(1)}, s32[8,128]{1,0:T(8,128)S(1)}, f32[8,128]{1,0:T(8,128)S(1)}) custom-call(s32[8]{0:T(128)} %packing_ref.1, bf16[768]{0:T(1024)(128)(2,1)} %token_ref.1, bf16[768]{0:T(1024)(128)(2,1)} %gain_hbm.1, ...), custom_call_target="tpu_custom_call" | custom-call | tf_op jit(solution)/shard_map/spread/pallas_call | solution.py:382
  48.9 0.0 copy-start
  48.9 0.0 copy-start.1
  48.9 0.0 copy-start.2
  48.9 0.0 copy-start.3
  48.9 0.0 copy-start.4
  48.9 24.9 %attend.1.att_ref = bf16[32,48,128]{2,1,0:T(8,128)(2,1)S(1)} custom-call(s32[8,128]{1,0:T(8,128)S(1)} %get-tuple-element.10.total_ref, f32[8,128]{1,0:T(8,128)S(1)} %get-tuple-element.11.norm_ref, bf16[32,48,128]{2,1,0:T(8,128)(2,1)S(1)} %get-tuple-element.12.q_ref, bf16[3,8,1024,128]{3,2,1,0:T(8,128)(2,1)S(1)} %get-tuple-element.13.k1, ...), custom_call_target="tpu_custom_call" | custom-call | tf_op jit(solution)/shard_map/attend/pallas_call | solution.py:522
  73.9 0.0 copy-done
  73.9 0.0 copy-done.1
  73.9 0.0 copy-done.2
  73.9 0.0 copy-done.3
  73.9 0.0 copy-done.4
  73.9 26.7 %finish.1 = bf16[256,768]{1,0:T(8,128)(2,1)S(1)} custom-call(s32[8]{0:T(128)S(1)} %copy-done.4, bf16[32,48,128]{2,1,0:T(8,128)(2,1)S(1)} %attend.1.att_ref, bf16[256,768]{1,0:T(8,128)(2,1)S(1)} %copy-done, s32[1,256]{1,0:T(1,128)S(1)} %bitcast.4, bf16[768]{0:T(1024)(128)(2,1)S(1)} %copy-done.2, bf16[768,768]{1,0:T(8,128)(2,1)S(1)} %copy-done.1), custom_call_target="tpu_custom_call" | custom-call | tf_op jit(solution)/shard_map/finish/pallas_call | solution.py:599
  100.7 0.7 copy.12
Async XLA Ops:
  48.9 25.0 %copy-start = (bf16[256,768]{1,0:T(8,128)(2,1)S(1)}, bf16[256,768]{1,0:T(8,128)(2,1)}, u32[]{:S(2)}) copy-start(bf16[256,768]{1,0:T(8,128)(2,1)} %series_ref.1) | copy-start | bytes 1179652
  48.9 25.0 %copy-start.1 = (bf16[768,768]{1,0:T(8,128)(2,1)S(1)}, bf16[768,768]{1,0:T(8,128)(2,1)}, u32[]{:S(2)}) copy-start(bf16[768,768]{1,0:T(8,128)(2,1)} %w_ref.1) | copy-start | bytes 3538948
  48.9 25.0 %copy-start.2 = (bf16[768]{0:T(1024)(128)(2,1)S(1)}, bf16[768]{0:T(1024)(128)(2,1)}, u32[]{:S(2)}) copy-start(bf16[768]{0:T(1024)(128)(2,1)} %token_ref.1) | copy-start | bytes 4612
  48.9 25.0 %copy-start.3 = (s32[256]{0:T(256)S(1)}, s32[256]{0:T(256)}, u32[]{:S(2)}) copy-start(s32[256]{0:T(256)} %param.11) | copy-start | bytes 3076
  48.9 25.0 %copy-start.4 = (s32[8]{0:T(128)S(1)}, s32[8]{0:T(128)}, u32[]{:S(2)}) copy-start(s32[8]{0:T(128)} %packing_ref.1) | copy-start | bytes 100

commit v7 on v6

--- a/solution.py
+++ b/solution.py
@@ -200,7 +200,7 @@
             send_kv(other(i, yy), i).start()
         return carry
 
-    lax.fori_loop(1, 5, start_plane, 0)
+    lax.fori_loop(1, 3, start_plane, 0)
     pack_queries(q_ref, project(2, wq) * SCALE)
     own_q.start()
 
@@ -289,9 +289,10 @@
         device_id=(partner, c), device_id_type=MESH,
     ).wait_recv()
     send_own(0)
-    lax.fori_loop(5, N_Z, start_plane, 0)
+    lax.fori_loop(3, 6, start_plane, 0)
     arrive_plane(1)
     send_own(1)
+    lax.fori_loop(6, N_Z, start_plane, 0)
     send_near(0)
     for yy in range(1, N_Y):
         send_q(other(0, yy)).start()

time: 103 us -> 105 us (1.019); the launches traced: 101 us -> 105 us
  Pallas kernels: 101 us -> 104 us
    pallas_call x1, Pallas kernels: 24.9 us -> 35.3 us  [attend(): pl.pallas_call(attend_kernel, out_shape=jax.ShapeDtypeStruct((N_CTX, QROW...]
    pallas_call x1, Pallas kernels: 26.7 us -> 17.4 us  [finish(): pl.pallas_call(finish_kernel, out_shape=jax.ShapeDtypeStruct(series.shape...]
    pallas_call x1, Pallas kernels: 48.9 us -> 51.2 us  [spread(): pl.pallas_call(spread_kernel, out_shape=(jax.ShapeDtypeStruct((PER, N_GRO...]
where the time goes in v7:
time: 105 us
  Pallas kernels  104 us (99%)
    pallas_call x1, Pallas kernels, spread(): pl.pallas_call(spread_kernel, out_shape=(jax.ShapeDtypeStruct((PER, N_GRO...  51.2 us
    pallas_call x1, Pallas kernels, attend(): pl.pallas_call(attend_kernel, out_shape=jax.ShapeDtypeStruct((N_CTX, QROW...  35.3 us
    pallas_call x1, Pallas kernels, finish(): pl.pallas_call(finish_kernel, out_shape=jax.ShapeDtypeStruct(series.shape...  17.4 us

profile of v7, /device:TPU:1, one launch (start us, length us, event | category | flops | bytes accessed | tf_op | source)
XLA Modules:
  0.0 104.8 jit_solution(4225614265876589271)
XLA Ops:
  0.0 51.2 %spread.1 = (bf16[3,8,1024,128]{3,2,1,0:T(8,128)(2,1)S(1)}, bf16[3,8,80,1024]{3,2,1,0:T(8,128)(2,1)S(1)}, bf16[32,48,128]{2,1,0:T(8,128)(2,1)S(1)}, s32[8,128]{1,0:T(8,128)S(1)}, f32[8,128]{1,0:T(8,128)S(1)}) custom-call(s32[8]{0:T(128)} %packing_ref.1, bf16[768]{0:T(1024)(128)(2,1)} %token_ref.1, bf16[768]{0:T(1024)(128)(2,1)} %gain_hbm.1, ...), custom_call_target="tpu_custom_call" | custom-call | tf_op jit(solution)/shard_map/spread/pallas_call | solution.py:383
  51.2 0.0 copy-start
  51.2 0.0 copy-start.1
  51.2 0.0 copy-start.2
  51.2 0.0 copy-start.3
  51.2 0.0 copy-start.4
  51.3 35.3 %attend.1.att_ref = bf16[32,48,128]{2,1,0:T(8,128)(2,1)S(1)} custom-call(s32[8,128]{1,0:T(8,128)S(1)} %get-tuple-element.10.total_ref, f32[8,128]{1,0:T(8,128)S(1)} %get-tuple-element.11.norm_ref, bf16[32,48,128]{2,1,0:T(8,128)(2,1)S(1)} %get-tuple-element.12.q_ref, bf16[3,8,1024,128]{3,2,1,0:T(8,128)(2,1)S(1)} %get-tuple-element.13.k1, ...), custom_call_target="tpu_custom_call" | custom-call | tf_op jit(solution)/shard_map/attend/pallas_call | solution.py:523
  86.6 0.0 copy-done
  86.6 0.0 copy-done.1
  86.6 0.0 copy-done.2
  86.6 0.0 copy-done.3
  86.6 0.0 copy-done.4
  86.6 17.4 %finish.1 = bf16[256,768]{1,0:T(8,128)(2,1)S(1)} custom-call(s32[8]{0:T(128)S(1)} %copy-done.4, bf16[32,48,128]{2,1,0:T(8,128)(2,1)S(1)} %attend.1.att_ref, bf16[256,768]{1,0:T(8,128)(2,1)S(1)} %copy-done, s32[1,256]{1,0:T(1,128)S(1)} %bitcast.4, bf16[768]{0:T(1024)(128)(2,1)S(1)} %copy-done.2, bf16[768,768]{1,0:T(8,128)(2,1)S(1)} %copy-done.1), custom_call_target="tpu_custom_call" | custom-call | tf_op jit(solution)/shard_map/finish/pallas_call | solution.py:600
  104.1 0.7 copy.12
Async XLA Ops:
  51.2 35.4 %copy-start = (bf16[256,768]{1,0:T(8,128)(2,1)S(1)}, bf16[256,768]{1,0:T(8,128)(2,1)}, u32[]{:S(2)}) copy-start(bf16[256,768]{1,0:T(8,128)(2,1)} %series_ref.1) | copy-start | bytes 1179652
  51.2 35.4 %copy-start.1 = (bf16[768,768]{1,0:T(8,128)(2,1)S(1)}, bf16[768,768]{1,0:T(8,128)(2,1)}, u32[]{:S(2)}) copy-start(bf16[768,768]{1,0:T(8,128)(2,1)} %w_ref.1) | copy-start | bytes 3538948
  51.2 35.4 %copy-start.2 = (bf16[768]{0:T(1024)(128)(2,1)S(1)}, bf16[768]{0:T(1024)(128)(2,1)}, u32[]{:S(2)}) copy-start(bf16[768]{0:T(1024)(128)(2,1)} %token_ref.1) | copy-start | bytes 4612
  51.2 35.4 %copy-start.3 = (s32[256]{0:T(256)S(1)}, s32[256]{0:T(256)}, u32[]{:S(2)}) copy-start(s32[256]{0:T(256)} %param.11) | copy-start | bytes 3076
  51.2 35.4 %copy-start.4 = (s32[8]{0:T(128)S(1)}, s32[8]{0:T(128)}, u32[]{:S(2)}) copy-start(s32[8]{0:T(128)} %packing_ref.1) | copy-start | bytes 100
